TPU v7x, 32 devices: a whole 2x2x4 slice. The times are simulated.
32 devices in a mesh: dp: 8 (over z, y), shard: 4 (over x, core).
Axes of the slice: x: 2, y: 2, z: 4, core: 2. Of those that a mesh axis runs over, the one named last changes fastest.
Arguments:
- tokens: bfloat16 [4096, 768], P(('dp', 'shard')), may hold values from -6 to 6
- cotangent: bfloat16 [4096, 768], P(('dp', 'shard')), may hold values from -6 to 6
- seq_ids: int32 [4096], P(('dp', 'shard')), may hold values from -1 to 127, as said below
- params: float32 [3768320], P(('dp', 'shard')), as said below
- first_moment: float32 [3768320], P(('dp', 'shard')), may hold values from -60 to 60
- second_moment: float32 [3768320], P(('dp', 'shard')), may hold values from 1 to 20
- step_count: int32 [1], replicated, may hold values from 1 to 20
Outputs:
- block_out: bfloat16 [4096, 768], P(('dp', 'shard'))
- grad_input: float32 [4096, 768], P(('dp', 'shard'))
- weight_grads: float32 [3768320], P(('dp', 'shard'))
- new_params: float32 [3768320], P(('dp', 'shard'))
- new_first_moment: float32 [3768320], P(('dp', 'shard'))
- new_second_moment: float32 [3768320], P(('dp', 'shard'))
Inputs may be any that keep to these rules, and one draw needn't show every extreme that they name: `seq_ids`: numbering restarts on every device's 128 slots: a device's first slot starts a sequence, consecutive equal numbers form one sequence, live slots come first and the remaining ones are -1. A sequence has at most 128 slots; some device holds exactly one such sequence, and some device has every slot live as a sequence of its own. `params`: entries are laid out as in the first step of the statement.
All inputs are finite; a program needn't handle non-finite values.
Results may differ from a plain program's by a relative error of at most 0.01.
Values may be sent and summed in bfloat16 or wider, within the bound.
A program may use at most 128 MiB of HBM per device.

v0:
```python
import functools
import math

import jax
import jax.numpy as jnp
from jax import lax
from jax.experimental import pallas as pl
from jax.experimental.pallas import tpu as pltpu
from jax.sharding import PartitionSpec as P

D = 768
HEADS = 24
HEAD_DIM = 64
STATE = 128
KERNEL = 4
STRETCH = 128
INNER = 1536
CHANNELS = 1792
LANES = 128
CUTS = 4
MESH = pl.DeviceIdType.MESH
PACKED = D + D * (INNER + CHANNELS) + D * HEADS + (KERNEL + 1) * CHANNELS + 3 * HEADS + INNER + INNER * D


EPS = 1e-05
BETA_ONE = 0.9
BETA_TWO = 0.999
ADAM_EPS = 1e-08
LEARN_RATE = 0.01
WEIGHT_DECAY = 0.1


def matmul(left, right):
    return jnp.dot(left, right, preferred_element_type=jnp.float32)


def over_rows(left, right):
    return lax.dot_general(
        left, right, (((0,), (0,)), ((), ())), preferred_element_type=jnp.float32
    )


def against(left, right):
    return lax.dot_general(
        left, right, (((1,), (1,)), ((), ())), preferred_element_type=jnp.float32
    )


def unpack(flat):
    shapes = [
        (D,),
        (D, INNER + CHANNELS),
        (D, HEADS),
        (KERNEL, CHANNELS),
        (CHANNELS,),
        (HEADS,),
        (HEADS,),
        (HEADS,),
        (INNER,),
        (INNER, D),
    ]
    pieces = []
    offset = 0
    for shape in shapes:
        length = math.prod(shape)
        pieces.append(flat[offset : offset + length].reshape(shape))
        offset = offset + length
    return pieces


ROWS_GAIN = D // LANES
ROWS_MAIN = D * (INNER + CHANNELS) // LANES
START_SMALL = ROWS_GAIN + ROWS_MAIN
START_OUT = (PACKED - INNER * D) // LANES
SHIFT = (PACKED - INNER * D) % LANES
ROWS_OUT = INNER * D // LANES
ROWS_SMALL = START_OUT + 1 - START_SMALL
WIDE = (INNER + CHANNELS) // LANES
THIN = D // LANES


def pack_kernel(gain_ref, small_ref, normed_ref, proj_ref, hidden_ref, cot_ref, out_ref, main, tail):
    main[0:ROWS_GAIN, :] = gain_ref[...]
    main[START_SMALL : START_OUT, :] = small_ref[0 : ROWS_SMALL - 1, :]
    tail[7:8, :] = small_ref[ROWS_SMALL - 1 : ROWS_SMALL, :]
    tail[8 + ROWS_OUT :, :] = jnp.zeros((tail.shape[0] - 8 - ROWS_OUT, LANES), jnp.float32)
    for pair in range(WIDE // 2):
        both = over_rows(normed_ref[...], proj_ref[:, pair * 2 * LANES : (pair + 1) * 2 * LANES])
        for side in range(2):
            main[pl.ds(ROWS_GAIN + 2 * pair + side, D, stride=WIDE), :] = both[
                :, side * LANES : (side + 1) * LANES
            ]
    for pair in range(THIN // 2):
        both = over_rows(hidden_ref[...], cot_ref[:, pair * 2 * LANES : (pair + 1) * 2 * LANES])
        for side in range(2):
            part = pltpu.roll(both[:, side * LANES : (side + 1) * LANES], SHIFT, 1)
            tail[pl.ds(8 + 2 * pair + side, INNER, stride=THIN), :] = part
    edge = START_OUT // 16 * 16

    def cast_main(step, carry):
        place = pl.multiple_of(step * 32, 32)
        out_ref[pl.ds(place, 32), :] = main[pl.ds(place, 32), :].astype(jnp.bfloat16)
        return carry

    lax.fori_loop(0, edge // 32, cast_main, 0)
    early = lax.broadcasted_iota(jnp.int32, (8, LANES), 1) < SHIFT
    seam = jnp.where(early, tail[7:15, :], tail[8:16, :])
    out_ref[edge : edge + 16, :] = jnp.concatenate([main[edge : edge + 8, :], seam], 0).astype(
        jnp.bfloat16
    )
    early_two = lax.broadcasted_iota(jnp.int32, (16, LANES), 1) < SHIFT

    def cast_tail(step, carry):
        place = pl.multiple_of(step * 16, 16)
        block = tail[pl.ds(pl.multiple_of(place + 16, 8), 16), :]
        before = tail[pl.ds(pl.multiple_of(place + 8, 8), 16), :]
        joined = jnp.concatenate([before[7:8], block[:15]], 0)
        out_ref[pl.ds(pl.multiple_of(edge + 16 + place, 16), 16), :] = jnp.where(
            early_two, joined, block
        ).astype(jnp.bfloat16)
        return carry

    lax.fori_loop(0, (out_ref.shape[0] - edge - 16) // 16, cast_tail, 0)


def pack_all(gain, small, normed, proj, hidden, cot, rows):
    vmem = pl.BlockSpec(memory_space=pltpu.VMEM)
    return pl.pallas_call(
        pack_kernel,
        out_shape=jax.ShapeDtypeStruct((rows, LANES), jnp.bfloat16),
        in_specs=[vmem] * 6,
        out_specs=vmem,
        scratch_shapes=[
            pltpu.VMEM((START_OUT, LANES), jnp.float32),
            pltpu.VMEM((rows - START_OUT + 16, LANES), jnp.float32),
        ],
        compiler_params=pltpu.CompilerParams(vmem_limit_bytes=48 * 1024 * 1024),
    )(gain, small, normed, proj, hidden, cot)


def scatter_kernel(grid, cuts, data, out, send_sem, recv_sem, *refs):
    deep, tall, wide = grid
    dp, shard = lax.axis_index("dp"), lax.axis_index("shard")
    z, y = lax.div(dp, tall), lax.rem(dp, tall)
    x, c = lax.div(shard, 2), lax.rem(shard, 2)

    def place(z, y, x, c):
        return (z * tall + y, x * 2 + c)

    xs = [lax.rem(x + j, wide) for j in range(1, wide)]
    ys = [lax.rem(y + j, tall) for j in range(1, tall)]
    zs = [lax.rem(z + j, deep) for j in range(1, deep)]
    to_x = [place(z, y, p, c) for p in xs]
    to_y = [place(z, p, x, c) for p in ys]
    to_z = [place(p, y, x, c) for p in zs]
    partner = place(z, y, x, 1 - c)
    everyone = [partner] + to_x + to_y + to_z
    barrier = pltpu.get_barrier_semaphore()
    for peer in everyone:
        pl.semaphore_signal(barrier, inc=1, device_id=peer, device_id_type=MESH)
    pl.semaphore_wait(barrier, len(everyone))

    sent = []

    def push(chunk, number, src, dst, peer):
        copy = pltpu.make_async_remote_copy(
            src_ref=src,
            dst_ref=dst,
            send_sem=send_sem.at[chunk, number],
            recv_sem=recv_sem.at[chunk, number],
            device_id=peer,
            device_id_type=MESH,
        )
        copy.start()
        sent.append(copy)
        return copy

    def total(parts):
        value = parts[0].astype(jnp.float32)
        for part in parts[1:]:
            value = value + part.astype(jnp.float32)
        return value

    first_x, first_y, first_z = 1, wide, wide + tall - 1
    chunks = [refs[i * 7 : i * 7 + 7] for i in range(len(cuts))]
    flights = []
    for k, (start, size) in enumerate(cuts):
        src = data.at[:, :, :, 1 - c, start : start + size]
        flights.append([push(k, 0, src, chunks[k][0], partner)])
    for k, (start, size) in enumerate(cuts):
        got, acc, got_one = chunks[k][:3]
        for copy in flights[k]:
            copy.wait_recv()

        def add(step, carry):
            zi, rest = lax.div(step, tall * wide), lax.rem(step, tall * wide)
            yi, xi = lax.div(rest, wide), lax.rem(rest, wide)
            mine = data[zi, yi, xi, c, start : start + size, :]
            acc[zi, yi, xi] = total([mine, got[zi, yi, xi]]).astype(jnp.bfloat16)
            return carry

        lax.fori_loop(0, deep * tall * wide, add, 0)
        flights[k] = []
        if k % 2 == 0:
            for j, p in enumerate(xs):
                flights[k].append(push(k, first_x + j, acc.at[:, :, p], got_one.at[j], to_x[j]))
        else:
            for j, p in enumerate(ys):
                flights[k].append(push(k, first_y + j, acc.at[:, p], got_one.at[j], to_y[j]))
    for k, (start, size) in enumerate(cuts):
        got, acc, got_one, acc_two, got_two = chunks[k][:5]
        for copy in flights[k]:
            copy.wait_recv()
        other = tall if k % 2 == 0 else wide

        def add(step, carry):
            zi, oi = lax.div(step, other), lax.rem(step, other)
            mine = acc[zi, oi, x] if k % 2 == 0 else acc[zi, y, oi]
            parts = [mine] + [got_one[j, zi, oi] for j in range(got_one.shape[0])]
            acc_two[zi, oi] = total(parts).astype(jnp.bfloat16)
            return carry

        lax.fori_loop(0, deep * other, add, 0)
        flights[k] = []
        if k % 2 == 0:
            for j, p in enumerate(ys):
                flights[k].append(push(k, first_y + j, acc_two.at[:, p], got_two.at[j], to_y[j]))
        else:
            for j, p in enumerate(xs):
                flights[k].append(push(k, first_x + j, acc_two.at[:, p], got_two.at[j], to_x[j]))
    for k, (start, size) in enumerate(cuts):
        acc_two, got_two, acc_three, got_three = chunks[k][3:]
        for copy in flights[k]:
            copy.wait_recv()
        mine = y if k % 2 == 0 else x

        def add(zi, carry):
            parts = [acc_two[zi, mine]] + [got_two[j, zi] for j in range(got_two.shape[0])]
            acc_three[zi] = total(parts).astype(jnp.bfloat16)
            return carry

        lax.fori_loop(0, deep, add, 0)
        flights[k] = []
        for j, p in enumerate(zs):
            flights[k].append(push(k, first_z + j, acc_three.at[p], got_three.at[j], to_z[j]))
    for k, (start, size) in enumerate(cuts):
        acc_three, got_three = chunks[k][5:]
        for copy in flights[k]:
            copy.wait_recv()
        parts = [acc_three[z]] + [got_three[j] for j in range(deep - 1)]
        out[start : start + size, :] = total(parts)
    for copy in sent:
        copy.wait_send()


def scatter_sum(flat, group_count, wide_count, rows):
    wide = group_count // 2
    tall = wide if wide_count % wide == 0 else 1
    deep = wide_count // tall
    step = -(-rows // (CUTS * 16)) * 16
    cuts = [(start, min(step, rows - start)) for start in range(0, rows, step)]
    scratch = []
    for k, (start, size) in enumerate(cuts):
        lead, other = (wide, tall) if k % 2 == 0 else (tall, wide)
        for shape in (
            (deep, tall, wide),
            (deep, tall, wide),
            (lead - 1, deep, other),
            (deep, other),
            (other - 1, deep),
            (deep,),
            (deep - 1,),
        ):
            scratch.append(pltpu.VMEM((*shape, size, LANES), jnp.bfloat16))
    peers = wide + tall + deep - 2
    sems = pltpu.SemaphoreType.DMA((len(cuts), peers))
    vmem = pl.BlockSpec(memory_space=pltpu.VMEM)
    return pl.pallas_call(
        functools.partial(scatter_kernel, (deep, tall, wide), cuts),
        out_shape=jax.ShapeDtypeStruct((rows, LANES), jnp.float32),
        in_specs=[vmem],
        out_specs=vmem,
        scratch_shapes=[sems, sems] + scratch,
        compiler_params=pltpu.CompilerParams(
            collective_id=0, has_side_effects=True, vmem_limit_bytes=56 * 1024 * 1024
        ),
    )(flat.reshape(deep, tall, wide, 2, rows, LANES))


def norm_in(inputs, gain):
    scale = lax.rsqrt(jnp.mean(inputs * inputs, axis=-1, keepdims=True) + EPS)
    return inputs * scale * gain


def lag_masks(seq_ids):
    padded = jnp.concatenate([jnp.full((KERNEL - 1,), -3, jnp.int32), seq_ids])
    masks = []
    for lag in range(1, KERNEL):
        earlier = padded[KERNEL - 1 - lag : KERNEL - 1 - lag + seq_ids.shape[0]]
        masks.append((earlier == seq_ids).astype(jnp.float32)[:, None])
    return masks


def state_space(values, bmat, cmat, steps_dt, rate, seq_ids):
    rows = values.shape[0]
    number = rows // STRETCH
    seg_blocks = seq_ids.reshape(number, STRETCH)
    before = jnp.concatenate([jnp.full((1,), -3, jnp.int32), seg_blocks[:-1, -1]])
    places = jnp.arange(STRETCH, dtype=jnp.int32)
    lower = places[:, None] >= places[None, :]

    def advance(state, pieces):
        x_block, b_block, c_block, dt_block, seg_block, prior = pieces
        logs = jnp.cumsum(dt_block * rate, axis=0)
        same = lower & (seg_block[:, None] == seg_block[None, :])
        spans = logs.T[:, :, None] - logs.T[:, None, :]
        factor = jnp.exp(jnp.where(same[None], spans, -1e30))
        scores = jnp.dot(c_block, b_block.T, precision=lax.Precision.HIGHEST)
        mixing = factor * scores[None] * dt_block.T[:, None, :]
        inside = jnp.einsum("htu,uhp->thp", mixing, x_block, precision=lax.Precision.HIGHEST)
        entering = jnp.exp(logs) * (seg_block == prior).astype(logs.dtype)[:, None]
        carried = (
            jnp.einsum("tn,hnp->thp", c_block, state, precision=lax.Precision.HIGHEST)
            * entering[:, :, None]
        )
        tail_mask = (seg_block == seg_block[-1]).astype(logs.dtype)[:, None]
        towards = jnp.exp(logs[-1][None, :] - logs) * dt_block * tail_mask
        fresh = jnp.einsum(
            "th,tn,thp->hnp", towards, b_block, x_block, precision=lax.Precision.HIGHEST
        )
        kept = jnp.exp(logs[-1]) * (seg_block[-1] == prior).astype(logs.dtype)
        return (fresh + kept[:, None, None] * state, inside + carried)

    initial = jnp.zeros((HEADS, STATE, HEAD_DIM), values.dtype)
    inputs = (
        values.reshape(number, STRETCH, HEADS, HEAD_DIM),
        bmat.reshape(number, STRETCH, STATE),
        cmat.reshape(number, STRETCH, STATE),
        steps_dt.reshape(number, STRETCH, HEADS),
        seg_blocks,
        before,
    )
    final_state, outputs = lax.scan(advance, initial, inputs)
    return outputs.reshape(rows, HEADS, HEAD_DIM)


def mixer(
    proj, dt_raw, conv_weight, conv_bias, dt_bias, a_log, d_skip, gain_out, lag_list, seq_ids
):
    rows = proj.shape[0]
    gate = proj[:, :INNER]
    conv_in = proj[:, INNER:]
    convolved = conv_bias + conv_weight[KERNEL - 1] * conv_in
    for lag in range(1, KERNEL):
        shifted = jnp.concatenate(
            [jnp.zeros((lag, conv_in.shape[1]), conv_in.dtype), conv_in[:-lag]]
        )
        convolved = convolved + conv_weight[KERNEL - 1 - lag] * shifted * lag_list[lag - 1]
    active = jax.nn.silu(convolved)
    values = active[:, :INNER].reshape(rows, HEADS, HEAD_DIM)
    bmat = active[:, INNER : INNER + STATE]
    cmat = active[:, INNER + STATE :]
    steps_dt = jax.nn.softplus(dt_raw + dt_bias)
    scanned = state_space(values, bmat, cmat, steps_dt, -jnp.exp(a_log), seq_ids)
    scanned = scanned + d_skip[None, :, None] * values
    gated = scanned.reshape(rows, INNER) * jax.nn.silu(gate)
    scale = lax.rsqrt(jnp.mean(gated * gated, axis=-1, keepdims=True) + EPS)
    return gated * scale * gain_out


def partial_mixer(masks, seq_ids):

    def apply_mixer(proj, dt_raw, conv_weight, conv_bias, dt_bias, a_log, d_skip, gain_out):
        return mixer(
            proj, dt_raw, conv_weight, conv_bias, dt_bias, a_log, d_skip, gain_out, masks, seq_ids
        )

    return apply_mixer


def block_pass(tokens, cotangent, seq_ids, weights, total):
    gain_in, w_main, w_dt, conv_w, conv_b, dt_bias, a_log, d_skip, gain_out, w_out = weights
    small = [
        piece.astype(jnp.float32) for piece in (conv_w, conv_b, dt_bias, a_log, d_skip, gain_out)
    ]
    inputs = tokens.astype(jnp.float32)
    normed_full, norm_back = jax.vjp(norm_in, inputs, gain_in.astype(jnp.float32))
    normed = normed_full.astype(jnp.bfloat16)
    proj = matmul(normed, w_main)
    dt_raw = matmul(normed, w_dt)
    masks = lag_masks(seq_ids)
    mixed_full, mixer_back = jax.vjp(partial_mixer(masks, seq_ids), proj, dt_raw, *small)
    hidden = mixed_full.astype(jnp.bfloat16)
    result = (inputs + matmul(hidden, w_out)).astype(jnp.bfloat16)
    live_cot = jnp.where(seq_ids[:, None] >= 0, cotangent, jnp.zeros_like(cotangent))
    grad_hidden = against(live_cot, w_out)
    backward = mixer_back(grad_hidden)
    grad_proj = backward[0].astype(jnp.bfloat16)
    grad_dt = backward[1].astype(jnp.bfloat16)
    grad_w_dt = over_rows(normed, grad_dt)
    grad_normed = against(grad_proj, w_main) + against(grad_dt, w_dt)
    grad_x, grad_gain = norm_back(grad_normed)
    grad_input = live_cot.astype(jnp.float32) + grad_x
    small_flat = jnp.concatenate([piece.reshape(-1) for piece in [grad_w_dt] + list(backward[2:])])
    small_flat = jnp.pad(small_flat, (0, ROWS_SMALL * LANES - small_flat.shape[0]))
    flat = pack_all(
        grad_gain.reshape(ROWS_GAIN, LANES),
        small_flat.reshape(ROWS_SMALL, LANES),
        normed,
        grad_proj,
        hidden,
        live_cot,
        total // LANES,
    )
    return (result, grad_input, flat)


def adamw(weight, first, second, grad, step_count):
    steps_done = step_count[0].astype(jnp.float32)
    first_new = BETA_ONE * first + (1.0 - BETA_ONE) * grad
    second_new = BETA_TWO * second + (1.0 - BETA_TWO) * grad * grad
    first_hat = first_new / (1.0 - jnp.power(BETA_ONE, steps_done))
    second_hat = second_new / (1.0 - jnp.power(BETA_TWO, steps_done))
    weight_new = weight - LEARN_RATE * (
        first_hat / (jnp.sqrt(second_hat) + ADAM_EPS) + WEIGHT_DECAY * weight
    )
    return (weight_new, first_new, second_new)


def per_device(tokens, cotangent, seq_ids, params, first_moment, second_moment, step_count):
    width = params.shape[0]
    rounded = params.astype(jnp.bfloat16)
    whole = lax.all_gather(rounded, ("dp", "shard"), axis=0, tiled=True)
    weights = unpack(whole)
    result, grad_input, flat = block_pass(tokens, cotangent, seq_ids, weights, whole.shape[0])
    owned = scatter_sum(flat, lax.axis_size("shard"), lax.axis_size("dp"), width // LANES)
    owned = owned.reshape(width)
    new_weight, new_first, new_second = adamw(
        params, first_moment, second_moment, owned, step_count
    )
    return (result, grad_input, owned, new_weight, new_first, new_second)


def solution(mesh):
    return jax.shard_map(
        per_device,
        mesh=mesh,
        in_specs=(
            P(("dp", "shard"), None),
            P(("dp", "shard"), None),
            P(("dp", "shard")),
            P(("dp", "shard")),
            P(("dp", "shard")),
            P(("dp", "shard")),
            P(),
        ),
        out_specs=(
            P(("dp", "shard"), None),
            P(("dp", "shard"), None),
            P(("dp", "shard")),
            P(("dp", "shard")),
            P(("dp", "shard")),
            P(("dp", "shard")),
        ),
        check_vma=False,
    )
```

profile of v0, /device:TPU:0, one launch (start us, length us, event | category | flops | bytes accessed | tf_op | source)
XLA Modules:
  0.0 280.6 jit_solution(14074505402128460731)
XLA Ops:
  7.2 1.7 convert_element_type.72
  9.7 1.2 slice.118
  10.9 1.0 fusion.47
  12.0 1.5 compare_convert_fusion
  13.6 0.8 fusion.60
  14.4 1.0 broadcast_select_fusion.cot_ref
  15.5 72.5 %all-gather.2.cloned.1.call-done = bf16[3768320]{0:T(1024)(128)(2,1)} async-done(((bf16[117760]{0:T(1024)(128)(2,1)}), bf16[3768320]{0:T(1024)(128)(2,1)}) %all-gather.2.cloned.1.call-update) | async-done | bytes 7536656 | tf_op jit(solution)/shard_map/all_gather | solution.py:433
  88.0 6.1 %slice.123 = bf16[2555904]{0:T(1024)(128)(2,1)} slice(bf16[3768320]{0:T(1024)(128)(2,1)} %all-gather.2.cloned.1.call-done), slice={[768:2556672]} | slice | bytes 10223616 | tf_op jit(solution)/shard_map/slice | solution.py:66
  94.1 10.3 %reshape.328 = bf16[768,3328]{1,0:T(8,128)(2,1)} reshape(bf16[2555904]{0:T(1024)(128)(2,1)} %slice.123) | data formatting | bytes 10223616 | tf_op jit(solution)/shard_map/reshape | solution.py:66
  104.4 0.7 slice_convert_fusion.3
  105.1 0.6 copy-done.31
  105.8 3.3 %fusion.98 = f32[128,3328]{1,0:T(8,128)S(1)} fusion(bf16[128,768]{1,0:T(8,128)(2,1)S(1)} %fusion.44.normed_ref, bf16[768,3328]{1,0:T(8,128)(2,1)} %reshape.328), kind=kOutput, calls=%fused_computation.171 | convolution fusion | flops 654311424 | bytes 7012352 | tf_op jit(solution)/shard_map/dot_general | solution.py:34
  109.4 0.8 slice_convert_fusion
  110.1 0.7 slice_convert_fusion.2
  110.9 1.7 fusion.23
  112.8 1.7 fusion.49
  114.5 1.0 slice.131
  115.5 0.8 slice_convert_fusion.4
  116.5 0.8 slice.132
  117.8 0.7 fusion.82
  119.1 0.8 exponential_multiply_fusion
  119.9 3.3 %slice.140 = bf16[1179648]{0:T(1024)(128)(2,1)} slice(bf16[3768320]{0:T(1024)(128)(2,1)} %all-gather.2.cloned.1.call-done), slice={[2585672:3765320]} | slice | bytes 4718592 | tf_op jit(solution)/shard_map/slice | solution.py:66
  123.2 5.4 %reshape.331 = bf16[1536,768]{1,0:T(8,128)(2,1)} reshape(bf16[1179648]{0:T(1024)(128)(2,1)} %slice.140) | data formatting | bytes 4718592 | tf_op jit(solution)/shard_map/reshape | solution.py:66
  128.6 2.3 copy.61
  130.9 3.0 %multiply_reduce_fusion.6 = (f32[128,24]{0,1:T(8,128)S(1)}, f32[128,24,64]{0,2,1:T(8,128)}) fusion(f32[128,24,64]{0,2,1:T(8,128)} %bitcast.87, f32[128,1792]{1,0:T(8,128)S(1)} %get-tuple-element.186), kind=kOutput, calls=%fused_computation.41 | convolution fusion | flops 302380032 | bytes 1650688 | tf_op jit(solution)/shard_map/transpose(jvp())/while/body/eval_jaxpr/th,tn,thp->hnp/dot_general | solution.py:328
  133.8 0.7 fusion.89
  134.5 4.1 %fusion.15 = f32[128,24,64]{0,2,1:T(8,128)} fusion(f32[128,24,64]{0,2,1:T(8,128)S(1)} %bitcast.90, f32[128,24,64]{0,2,1:T(8,128)S(1)} %bitcast.97, f32[24,128]{1,0:T(8,128)S(1)} %get-tuple-element.211, f32[128,128]{1,0:T(8,128)S(1)} %fusion.63, f32[24,128]{1,0:T(8,128)S(1)} %copy.63, pred[128,128]{1,0:T(8,128)(4,1)S(1)} %fusion.60, ...), kind=kOutput, calls=%fused_computation.13 | convolution fusion | flops 303955968 | bytes 2478080 | tf_op jit(solution)/shard_map/jvp()/while/body/eval_jaxpr/htu,uhp->thp/dot_general | solution.py:320
  138.7 2.3 copy.66
  141.0 1.6 multiply_reduce_fusion.11
  142.6 0.8 slice_convert_fusion.1
  143.4 1.5 multiply_reduce_fusion.7
  145.0 2.5 multiply_reduce_fusion.8
  147.5 2.3 copy.67
  149.8 1.6 multiply_reduce_fusion.9
  151.4 2.0 convolution_bitcast_fusion.1
  153.4 1.3 copy.71
  154.7 2.8 %fusion.18 = bf16[128,768]{1,0:T(8,128)(2,1)} fusion(bf16[128,1536]{1,0:T(8,128)(2,1)S(1)} %get-tuple-element.194.hidden_ref, bf16[1536,768]{1,0:T(8,128)(2,1)} %reshape.331, bf16[128,768]{1,0:T(8,128)(2,1)} %param.7), kind=kOutput, calls=%fused_computation.18 | convolution fusion | flops 302284800 | bytes 3145728 | tf_op jit(solution)/shard_map/dot_general | solution.py:34
  157.6 0.8 reduce_sum.263
  158.3 0.6 reduce_sum.267
  159.0 5.7 %fusion.20 = (f32[24,128]{1,0:T(8,128)S(1)}, f32[24,128]{1,0:T(8,128)S(1)}, f32[24,128]{1,0:T(8,128)}, f32[128,128]{1,0:T(8,128)}) fusion(f32[24,128]{1,0:T(8,128)} %copy-done.39, f32[128,128]{1,0:T(8,128)S(1)} %fusion.63, f32[24,128]{1,0:T(8,128)} %copy-done.40, pred[128,128]{1,0:T(8,128)(4,1)} %copy-done.38, f32[24,64,128]{2,1,0:T(8,128)} %bitcast.92, ...), kind=kOutput, calls=%fused_computation.25 | convolution fusion | flops 307076096 | bytes 1781760 | tf_op jit(solution)/shard_map/transpose(jvp())/while/body/eval_jaxpr/htu,uhp->thp/dot_general | solution.py:320
  164.9 2.0 reduce_window_sum.25
  166.9 0.9 copy.73
  167.8 2.1 fusion.93
  169.9 2.5 convolution_bitcast_fusion
  172.4 4.2 %fusion.12 = f32[128,24,64]{0,2,1:T(8,128)} fusion(f32[24,64,128]{2,1,0:T(8,128)} %bitcast.93, f32[128,24,64]{0,2,1:T(8,128)} %get-tuple-element.214, f32[24,128]{1,0:T(8,128)} %copy-done.39, f32[128,128]{1,0:T(8,128)} %copy-done.33, f32[24,128]{1,0:T(8,128)} %copy-done.40, pred[128,128]{1,0:T(8,128)(4,1)} %copy-done.38, f32[128,24]{0,1:T(8,128)S(1)} %get-tuple-element.199), kind=kOutput, calls=%fused_computation.12 | convolution fusion | flops 303955968 | bytes 2478080 | tf_op jit(solution)/shard_map/transpose(jvp())/while/body/eval_jaxpr/htu,uhp->thp/dot_general | solution.py:320
  176.9 0.3 convolution_add_fusion.2
  177.2 1.4 copy.70
  178.6 1.4 multiply_add_fusion.2
  180.3 1.5 multiply_reduce_fusion.5
  181.9 1.7 multiply_reduce_fusion.4
  183.6 1.0 fusion.76
  184.6 1.2 reshape.336
  185.8 1.4 slice_multiply_fusion.1
  187.6 1.4 fusion.90
  189.1 0.8 negate_multiply_fusion
  189.8 0.7 concatenate.19
  190.6 1.5 add_convert_fusion.proj_ref
  192.1 4.3 %fusion.99 = f32[128,768]{1,0:T(8,128)S(1)} fusion(bf16[128,3328]{1,0:T(8,128)(2,1)S(1)} %add_convert_fusion.proj_ref, bf16[768,3328]{1,0:T(8,128)(2,1)} %reshape.328), kind=kOutput, calls=%fused_computation.172 | convolution fusion | flops 654311424 | bytes 6356992 | tf_op jit(solution)/shard_map/dot_general | solution.py:44
  196.5 0.4 fusion.45
  196.9 13.3 %shard_map.118 = bf16[29440,128]{1,0:T(8,128)(2,1)} custom-call(f32[6,128]{1,0:T(8,128)S(1)} %bitcast.85, f32[227,128]{1,0:T(8,128)S(1)} %pad_bitcast_fusion.small_ref, bf16[128,768]{1,0:T(8,128)(2,1)S(1)} %fusion.44.normed_ref, bf16[128,3328]{1,0:T(8,128)(2,1)S(1)} %add_convert_fusion.proj_ref, bf16[128,1536]{1,0:T(8,128)(2,1)S(1)} %get-tuple-element.194.hidden_ref, ...), custom_call_target="tpu_custom_call" | custom-call | tf_op jit(solution)/shard_map/pallas_call | solution.py:128
  210.2 59.3 %shard_map.119 = f32[920,128]{1,0:T(8,128)} custom-call(bf16[4,2,2,2,920,128]{5,4,3,2,1,0:T(8,128)(2,1)} %bitcast.86), custom_call_target="tpu_custom_call" | custom-call | tf_op jit(solution)/shard_map/pallas_call | solution.py:278
  269.6 0.9 fusion.46
  270.5 2.4 multiply_subtract_fusion
  272.9 0.8 copy.83
  (148 shorter events, 3.3 us)
Async XLA Ops:
  7.2 80.8 %all-gather.2.cloned.1.call-start = ((), (), s32[]{:S(2)}) async-start(), calls=%async_computation | async-start | bytes 7772160 | tf_op jit(solution)/shard_map/all_gather | solution.py:433
  12.0 2.4 copy-start.56
  12.0 93.1 %copy-start.43 = (f32[128]{0:T(128)}, f32[128]{0:T(128)S(1)}, u32[]{:S(2)}) copy-start(f32[128]{0:T(128)S(1)} %fusion.80) | copy-start | bytes 1540
  13.5 80.6 %copy-start.45 = (pred[128]{0:T(512)(128)(4,1)}, pred[128]{0:T(512)(128)(4,1)S(1)}, u32[]{:S(2)}) copy-start(pred[128]{0:T(512)(128)(4,1)S(1)} %get-tuple-element.206) | copy-start | bytes 388
  13.5 97.3 %copy-start.47 = (f32[128]{0:T(128)}, f32[128]{0:T(128)S(1)}, u32[]{:S(2)}) copy-start(f32[128]{0:T(128)S(1)} %get-tuple-element.208) | copy-start | bytes 1540
  13.6 97.3 %copy-start.49 = (f32[128]{0:T(128)}, f32[128]{0:T(128)S(1)}, u32[]{:S(2)}) copy-start(f32[128]{0:T(128)S(1)} %get-tuple-element.209) | copy-start | bytes 1540
  13.6 97.3 %copy-start.51 = (f32[128]{0:T(128)}, f32[128]{0:T(128)S(1)}, u32[]{:S(2)}) copy-start(f32[128]{0:T(128)S(1)} %get-tuple-element.207) | copy-start | bytes 1540
  13.6 120.2 %copy-start.41 = (f32[128]{0:T(128)}, f32[128]{0:T(128)S(1)}, u32[]{:S(2)}) copy-start(f32[128]{0:T(128)S(1)} %get-tuple-element.205) | copy-start | bytes 1540
  13.6 120.2 %copy-start.53 = (f32[128]{0:T(128)}, f32[128]{0:T(128)S(1)}, u32[]{:S(2)}) copy-start(f32[128]{0:T(128)S(1)} %get-tuple-element.210) | copy-start | bytes 1540
  14.4 120.1 %copy-start.38 = (pred[128,128]{1,0:T(8,128)(4,1)}, pred[128,128]{1,0:T(8,128)(4,1)S(1)}, u32[]{:S(2)}) copy-start(pred[128,128]{1,0:T(8,128)(4,1)S(1)} %fusion.60) | copy-start | bytes 49156
  94.1 11.6 %copy-start.10 = (bf16[128,768]{1,0:T(8,128)(2,1)S(1)}, bf16[128,768]{1,0:T(8,128)(2,1)}, u32[]{:S(2)}) copy-start(bf16[128,768]{1,0:T(8,128)(2,1)} %param.7) | copy-start | bytes 589828
  105.1 0.6 copy-start.31
  109.2 1.7 copy-start.5
  109.3 3.3 %copy-start.1 = (f32[126,1792]{1,0:T(8,128)}, f32[126,1792]{1,0:T(8,128)S(1)}, u32[]{:S(2)}) copy-start(f32[126,1792]{1,0:T(8,128)S(1)} %slice.128) | copy-start | bytes 2709508
  109.3 3.2 %copy-start.3 = (f32[127,1792]{1,0:T(8,128)}, f32[127,1792]{1,0:T(8,128)S(1)}, u32[]{:S(2)}) copy-start(f32[127,1792]{1,0:T(8,128)S(1)} %slice.126) | copy-start | bytes 2731012
  110.1 2.4 copy-start.25
  110.1 2.4 copy-start.27
  110.1 2.4 copy-start.29
  112.8 46.1 %copy-start.33 = (f32[128,128]{1,0:T(8,128)}, f32[128,128]{1,0:T(8,128)S(1)}, u32[]{:S(2)}) copy-start(f32[128,128]{1,0:T(8,128)S(1)} %fusion.63) | copy-start | bytes 196612
  117.6 5.6 %copy-start.18 = (bf16[768,24]{1,0:T(8,128)(2,1)}, bf16[768,24]{1,0:T(8,128)(2,1)S(1)}, u32[]{:S(2)}) copy-start(bf16[768,24]{1,0:T(8,128)(2,1)S(1)} %reshape.329) | copy-start | bytes 110596
  117.8 16.7 %copy-start.39 = (f32[24,128]{1,0:T(8,128)}, f32[24,128]{1,0:T(8,128)S(1)}, u32[]{:S(2)}) copy-start(f32[24,128]{1,0:T(8,128)S(1)} %get-tuple-element.211) | copy-start | bytes 36868
  118.6 4.6 %copy-start.55 = (f32[24]{0:T(128)}, f32[24]{0:T(128)S(1)}, u32[]{:S(2)}) copy-start(f32[24]{0:T(128)S(1)} %fusion.82) | copy-start | bytes 292
  119.1 15.5 %copy-start.40 = (f32[24,128]{1,0:T(8,128)}, f32[24,128]{1,0:T(8,128)S(1)}, u32[]{:S(2)}) copy-start(f32[24,128]{1,0:T(8,128)S(1)} %copy.63) | copy-start | bytes 36868
  130.8 3.7 %copy-start.7 = (f32[128,1536]{0,1:T(8,128)S(1)}, f32[128,1536]{0,1:T(8,128)}, u32[]{:S(2)}) copy-start(f32[128,1536]{0,1:T(8,128)} %copy.61) | copy-start | bytes 2359300
  130.9 3.7 %copy-start.16 = (f32[128,1536]{0,1:S(1)}, f32[128,1536]{0,1}, u32[]{:S(2)}) copy-start(f32[128,1536]{0,1} %fusion.49) | copy-start | bytes 2359300
  141.0 2.4 copy-start
  143.4 1.6 copy-start.9
  149.8 1.6 copy-start.8
  159.0 5.8 %copy-start.35 = (f32[1,24]{0,1:T(8,128)S(1)}, f32[1,24]{0,1:T(8,128)}, u32[]{:S(2)}) copy-start(f32[1,24]{0,1:T(8,128)} %get-tuple-element.201) | copy-start | bytes 292
  159.0 5.8 %copy-start.36 = (f32[1,24]{0,1:T(8,128)S(1)}, f32[1,24]{0,1:T(8,128)}, u32[]{:S(2)}) copy-start(f32[1,24]{0,1:T(8,128)} %copy.71) | copy-start | bytes 292
  159.0 5.8 %copy-start.42 = (f32[128]{0:T(128)S(1)}, f32[128]{0:T(128)}, u32[]{:S(2)}) copy-start(f32[128]{0:T(128)} %copy-done.41) | copy-start | bytes 1540
  159.0 5.8 %copy-start.54 = (f32[128]{0:T(128)S(1)}, f32[128]{0:T(128)}, u32[]{:S(2)}) copy-start(f32[128]{0:T(128)} %copy-done.53) | copy-start | bytes 1540
  172.4 4.3 %copy-start.23 = (f32[128,128]{1,0:T(8,128)S(1)}, f32[128,128]{1,0:T(8,128)}, u32[]{:S(2)}) copy-start(f32[128,128]{1,0:T(8,128)} %get-tuple-element.131) | copy-start | bytes 196612
  172.4 4.2 %copy-start.24 = (f32[128,128]{1,0:T(8,128)S(1)}, f32[128,128]{1,0:T(8,128)}, u32[]{:S(2)}) copy-start(f32[128,128]{1,0:T(8,128)} %convolution_bitcast_fusion.1) | copy-start | bytes 196612
  178.6 1.4 copy-start.6
  178.6 1.7 copy-start.13
  178.6 1.7 copy-start.52
  180.3 1.5 copy-start.2
  180.3 1.6 copy-start.4
  180.3 1.6 copy-start.48
  180.3 1.6 copy-start.50
  181.9 1.7 copy-start.34
  181.9 3.9 %copy-start.30 = (f32[1792]{0:T(1024)S(1)}, f32[1792]{0:T(1024)}, u32[]{:S(2)}) copy-start(f32[1792]{0:T(1024)} %copy-done.29) | copy-start | bytes 21508
  183.5 3.7 %copy-start.28 = (f32[1792]{0:T(1024)S(1)}, f32[1792]{0:T(1024)}, u32[]{:S(2)}) copy-start(f32[1792]{0:T(1024)} %copy-done.27) | copy-start | bytes 21508
  185.8 1.5 copy-start.15
  185.8 1.7 copy-start.14
  185.8 1.7 copy-start.26
  187.6 2.2 copy-start.37
  192.1 4.3 %copy-start.11 = (bf16[128,768]{1,0:T(8,128)(2,1)S(1)}, bf16[128,768]{1,0:T(8,128)(2,1)}, u32[]{:S(2)}) copy-start(bf16[128,768]{1,0:T(8,128)(2,1)} %param.7) | copy-start | bytes 589828
  192.1 4.3 %copy-start.19 = (bf16[768,24]{1,0:T(8,128)(2,1)S(1)}, bf16[768,24]{1,0:T(8,128)(2,1)}, u32[]{:S(2)}) copy-start(bf16[768,24]{1,0:T(8,128)(2,1)} %copy-done.18) | copy-start | bytes 110596
  192.1 4.3 %copy-start.32 = (f32[768]{0:T(1024)S(1)}, f32[768]{0:T(1024)}, u32[]{:S(2)}) copy-start(f32[768]{0:T(1024)} %copy-done.31) | copy-start | bytes 9220
  192.1 4.3 %copy-start.44 = (f32[128]{0:T(128)S(1)}, f32[128]{0:T(128)}, u32[]{:S(2)}) copy-start(f32[128]{0:T(128)} %copy-done.43) | copy-start | bytes 1540
  192.1 4.7 %copy-start.57 = (f32[128]{0:T(128)S(1)}, f32[128]{0:T(128)}, u32[]{:S(2)}) copy-start(f32[128]{0:T(128)} %copy-done.56) | copy-start | bytes 1540
  210.2 59.4 %copy-start.20 = (bf16[128,768]{1,0:T(8,128)(2,1)S(1)}, bf16[128,768]{1,0:T(8,128)(2,1)}, u32[]{:S(2)}) copy-start(bf16[128,768]{1,0:T(8,128)(2,1)} %param.8) | copy-start | bytes 589828
  210.2 59.4 %copy-start.46 = (pred[128]{0:T(512)(128)(4,1)S(1)}, pred[128]{0:T(512)(128)(4,1)}, u32[]{:S(2)}) copy-start(pred[128]{0:T(512)(128)(4,1)} %copy-done.45) | copy-start | bytes 388
  210.2 60.3 %copy-start.17 = (f32[117760]{0:T(1024)S(1)}, f32[117760]{0:T(1024)}, u32[]{:S(2)}) copy-start(f32[117760]{0:T(1024)} %param.10) | copy-start | bytes 1413124
  210.2 60.3 %copy-start.21 = (f32[117760]{0:T(1024)S(1)}, f32[117760]{0:T(1024)}, u32[]{:S(2)}) copy-start(f32[117760]{0:T(1024)} %param.12) | copy-start | bytes 1413124
  210.2 60.3 %copy-start.22 = (f32[117760]{0:T(1024)S(1)}, f32[117760]{0:T(1024)}, u32[]{:S(2)}) copy-start(f32[117760]{0:T(1024)} %param.11) | copy-start | bytes 1413124
  270.5 2.4 copy-start.12
Sparse Core Ops, SparseCore 0:
  11.4 76.4 all-gather.1
where the time goes:
time: 282 us; the launch traced here: 281 us
  Pallas kernels  72.6 us (26%)
  waiting for transfers between devices  72.5 us (26%)
  local copies, waits for them, and re-layouts  44.6 us (16%)
  other arithmetic  37.7 us (13%)
  matrix products  37.6 us (13%)
  between operations  15.4 us (5%)
    all_gather x1, waiting for transfers between devices, per_device(): whole = lax.all_gather(rounded, ('dp', 'shard'), axis=0, tiled=True)  72.5 us
    pallas_call x1, Pallas kernels, scatter_sum(): pl.pallas_call(functools.partial(scatter_kernel, (deep, tall, wide), cuts...  59.3 us
    reshape x3, local copies, waits for them, and re-layouts, unpack(): pieces.append(flat[offset:offset + length].reshape(shape))  16 us
    dot_general x3, matrix products, advance(): jnp.einsum('htu,uhp->thp', mixing, x_block, precision=lax.Precision.HIGHEST)  14.1 us
    pallas_call x1, Pallas kernels, pack_all(): pl.pallas_call(pack_kernel, out_shape=jax.ShapeDtypeStruct((rows, LANES),...  13.3 us
    slice x3, local copies, waits for them, and re-layouts, unpack(): pieces.append(flat[offset:offset + length].reshape(shape))  10.2 us
    dot_general x3, matrix products, matmul(): return jnp.dot(left, right, preferred_element_type=jnp.float32)  6.36 us
    dot_general x3, matrix products, against(): lax.dot_general(left, right, (((1,), (1,)), ((), ())), preferred_element_...  6.2 us
  transfers between devices with their start and end apart: 1, of which 1 were waited for; matrix products, arithmetic and copies ran while one was open for 2% of the time, Pallas kernels for 0%

commit v1 on v0

--- a/solution.py
+++ b/solution.py
@@ -17,7 +17,8 @@
 INNER = 1536
 CHANNELS = 1792
 LANES = 128
-CUTS = 4
+CUTS = 8
+SPAN = 256
 MESH = pl.DeviceIdType.MESH
 PACKED = D + D * (INNER + CHANNELS) + D * HEADS + (KERNEL + 1) * CHANNELS + 3 * HEADS + INNER + INNER * D
 
@@ -44,28 +45,6 @@
     return lax.dot_general(
         left, right, (((1,), (1,)), ((), ())), preferred_element_type=jnp.float32
     )
-
-
-def unpack(flat):
-    shapes = [
-        (D,),
-        (D, INNER + CHANNELS),
-        (D, HEADS),
-        (KERNEL, CHANNELS),
-        (CHANNELS,),
-        (HEADS,),
-        (HEADS,),
-        (HEADS,),
-        (INNER,),
-        (INNER, D),
-    ]
-    pieces = []
-    offset = 0
-    for shape in shapes:
-        length = math.prod(shape)
-        pieces.append(flat[offset : offset + length].reshape(shape))
-        offset = offset + length
-    return pieces
 
 
 ROWS_GAIN = D // LANES
@@ -77,6 +56,17 @@
 ROWS_SMALL = START_OUT + 1 - START_SMALL
 WIDE = (INNER + CHANNELS) // LANES
 THIN = D // LANES
+
+
+def in_spans(total, body):
+    def step(number, carry):
+        body(pl.multiple_of(number * SPAN, SPAN), SPAN)
+        return carry
+
+    whole = total // SPAN
+    lax.fori_loop(0, whole, step, 0)
+    if total % SPAN:
+        body(whole * SPAN, total - whole * SPAN)
 
 
 def pack_kernel(gain_ref, small_ref, normed_ref, proj_ref, hidden_ref, cot_ref, out_ref, main, tail):
@@ -97,30 +87,26 @@
             tail[pl.ds(8 + 2 * pair + side, INNER, stride=THIN), :] = part
     edge = START_OUT // 16 * 16
 
-    def cast_main(step, carry):
-        place = pl.multiple_of(step * 32, 32)
-        out_ref[pl.ds(place, 32), :] = main[pl.ds(place, 32), :].astype(jnp.bfloat16)
-        return carry
-
-    lax.fori_loop(0, edge // 32, cast_main, 0)
+    def cast_main(place, size):
+        out_ref[pl.ds(place, size), :] = main[pl.ds(place, size), :].astype(jnp.bfloat16)
+
+    in_spans(edge, cast_main)
     early = lax.broadcasted_iota(jnp.int32, (8, LANES), 1) < SHIFT
     seam = jnp.where(early, tail[7:15, :], tail[8:16, :])
     out_ref[edge : edge + 16, :] = jnp.concatenate([main[edge : edge + 8, :], seam], 0).astype(
         jnp.bfloat16
     )
-    early_two = lax.broadcasted_iota(jnp.int32, (16, LANES), 1) < SHIFT
-
-    def cast_tail(step, carry):
-        place = pl.multiple_of(step * 16, 16)
-        block = tail[pl.ds(pl.multiple_of(place + 16, 8), 16), :]
-        before = tail[pl.ds(pl.multiple_of(place + 8, 8), 16), :]
-        joined = jnp.concatenate([before[7:8], block[:15]], 0)
-        out_ref[pl.ds(pl.multiple_of(edge + 16 + place, 16), 16), :] = jnp.where(
-            early_two, joined, block
+
+    def cast_tail(place, size):
+        block = tail[pl.ds(place + 16, size), :]
+        before = tail[pl.ds(place + 8, size), :]
+        joined = jnp.concatenate([before[7:8], block[: size - 1]], 0)
+        lanes = lax.broadcasted_iota(jnp.int32, (size, LANES), 1)
+        out_ref[pl.ds(edge + 16 + place, size), :] = jnp.where(
+            lanes < SHIFT, joined, block
         ).astype(jnp.bfloat16)
-        return carry
-
-    lax.fori_loop(0, (out_ref.shape[0] - edge - 16) // 16, cast_tail, 0)
+
+    in_spans(out_ref.shape[0] - edge - 16, cast_tail)
 
 
 def pack_all(gain, small, normed, proj, hidden, cot, rows):
@@ -287,6 +273,162 @@
     )(flat.reshape(deep, tall, wide, 2, rows, LANES))
 
 
+def gather_kernel(grid, cuts, own, out, send_sem, recv_sem):
+    deep, tall, wide = grid
+    dp, shard = lax.axis_index("dp"), lax.axis_index("shard")
+    z, y = lax.div(dp, tall), lax.rem(dp, tall)
+    x, c = lax.div(shard, 2), lax.rem(shard, 2)
+
+    def place(z, y, x, c):
+        return (z * tall + y, x * 2 + c)
+
+    to_x = [place(z, y, lax.rem(x + j, wide), c) for j in range(1, wide)]
+    to_y = [place(z, lax.rem(y + j, tall), x, c) for j in range(1, tall)]
+    to_z = [place(lax.rem(z + j, deep), y, x, c) for j in range(1, deep)]
+    partner = place(z, y, x, 1 - c)
+    everyone = [partner] + to_x + to_y + to_z
+    barrier = pltpu.get_barrier_semaphore()
+    for peer in everyone:
+        pl.semaphore_signal(barrier, inc=1, device_id=peer, device_id_type=MESH)
+    pl.semaphore_wait(barrier, len(everyone))
+
+    sent = []
+
+    def push(chunk, number, src, dst, peers):
+        started = []
+        for j, peer in enumerate(peers):
+            copy = pltpu.make_async_remote_copy(
+                src_ref=src,
+                dst_ref=dst,
+                send_sem=send_sem.at[chunk, number + j],
+                recv_sem=recv_sem.at[chunk, number + j],
+                device_id=peer,
+                device_id_type=MESH,
+            )
+            copy.start()
+            started.append(copy)
+        sent.extend(started)
+        return started
+
+    first_x, first_y, first_z = 1, wide, wide + tall - 1
+    flights = []
+    for k, (start, size) in enumerate(cuts):
+        rows = pl.ds(start, size)
+        flights.append(push(k, first_z, own.at[rows], out.at[z, y, x, c, rows], to_z))
+    out[z, y, x, c] = own[...]
+    for k, (start, size) in enumerate(cuts):
+        rows = pl.ds(start, size)
+        for copy in flights[k]:
+            copy.wait_recv()
+        line = out.at[:, y, x, c, rows]
+        if k % 2 == 0:
+            flights[k] = push(k, first_y, line, line, to_y)
+        else:
+            flights[k] = push(k, first_x, line, line, to_x)
+    for k, (start, size) in enumerate(cuts):
+        rows = pl.ds(start, size)
+        for copy in flights[k]:
+            copy.wait_recv()
+        if k % 2 == 0:
+            sheet = out.at[:, :, x, c, rows]
+            flights[k] = push(k, first_x, sheet, sheet, to_x)
+        else:
+            sheet = out.at[:, y, :, c, rows]
+            flights[k] = push(k, first_y, sheet, sheet, to_y)
+    for k, (start, size) in enumerate(cuts):
+        for copy in flights[k]:
+            copy.wait_recv()
+        cube = out.at[:, :, :, c, pl.ds(start, size)]
+        flights[k] = push(k, 0, cube, cube, [partner])
+    for flight in flights:
+        for copy in flight:
+            copy.wait_recv()
+    for copy in sent:
+        copy.wait_send()
+
+
+def gather_rows(own, group_count, wide_count):
+    rows = own.shape[0]
+    wide = group_count // 2
+    tall = wide if wide_count % wide == 0 else 1
+    deep = wide_count // tall
+    step = -(-rows // (CUTS * 16)) * 16
+    cuts = [(start, min(step, rows - start)) for start in range(0, rows, step)]
+    sems = pltpu.SemaphoreType.DMA((len(cuts), wide + tall + deep - 2))
+    vmem = pl.BlockSpec(memory_space=pltpu.VMEM)
+    whole = pl.pallas_call(
+        functools.partial(gather_kernel, (deep, tall, wide), cuts),
+        out_shape=jax.ShapeDtypeStruct((deep, tall, wide, 2, rows, LANES), jnp.bfloat16),
+        in_specs=[vmem],
+        out_specs=vmem,
+        scratch_shapes=[sems, sems],
+        compiler_params=pltpu.CompilerParams(
+            collective_id=1, has_side_effects=True, vmem_limit_bytes=32 * 1024 * 1024
+        ),
+    )(own)
+    return whole.reshape(wide_count * group_count * rows, LANES)
+
+
+def unpack_kernel(rows_ref, main_ref, out_ref, main, tail):
+    edge = START_OUT // 16 * 16
+
+    def widen(place, size):
+        main[pl.ds(place, size), :] = rows_ref[pl.ds(place, size), :].astype(jnp.float32)
+
+    in_spans(main.shape[0], widen)
+
+    def widen_tail(place, size):
+        block = rows_ref[pl.ds(edge + place, size), :].astype(jnp.float32)
+        tail[pl.ds(place, size), :] = pltpu.roll(block, LANES - SHIFT, 1)
+
+    in_spans(tail.shape[0], widen_tail)
+    for j in range(WIDE):
+        main_ref[:, j * LANES : (j + 1) * LANES] = main[
+            pl.ds(ROWS_GAIN + j, D, stride=WIDE), :
+        ].astype(jnp.bfloat16)
+    early = lax.broadcasted_iota(jnp.int32, (INNER, LANES), 1) < LANES - SHIFT
+    base = START_OUT - edge
+    for j in range(THIN):
+        here = tail[pl.ds(base + j, INNER, stride=THIN), :]
+        after = tail[pl.ds(base + j + 1, INNER, stride=THIN), :]
+        out_ref[:, j * LANES : (j + 1) * LANES] = jnp.where(early, here, after).astype(
+            jnp.bfloat16
+        )
+
+
+def unpack(rows):
+    w_main, w_out = unpack_wide(rows)
+    gain_in = rows[:ROWS_GAIN].reshape(D)
+    flat = rows[START_SMALL : START_SMALL + ROWS_SMALL].reshape(-1)
+    shapes = [(D, HEADS), (KERNEL, CHANNELS), (CHANNELS,), (HEADS,), (HEADS,), (HEADS,), (INNER,)]
+    pieces = []
+    offset = 0
+    for shape in shapes:
+        length = math.prod(shape)
+        pieces.append(flat[offset : offset + length].reshape(shape))
+        offset = offset + length
+    return [gain_in, w_main] + pieces + [w_out]
+
+
+def unpack_wide(rows):
+    vmem = pl.BlockSpec(memory_space=pltpu.VMEM)
+    edge = START_OUT // 16 * 16
+    return pl.pallas_call(
+        unpack_kernel,
+        out_shape=(
+            jax.ShapeDtypeStruct((D, INNER + CHANNELS), jnp.bfloat16),
+            jax.ShapeDtypeStruct((INNER, D), jnp.bfloat16),
+        ),
+        in_specs=[vmem],
+        out_specs=(vmem, vmem),
+        scratch_shapes=[
+            pltpu.VMEM((-(-START_SMALL // 32) * 32, LANES), jnp.float32),
+            pltpu.VMEM(((rows.shape[0] - edge) // 32 * 32, LANES), jnp.float32),
+        ],
+        compiler_params=pltpu.CompilerParams(vmem_limit_bytes=48 * 1024 * 1024),
+    )(rows)
+
+
 def norm_in(inputs, gain):
     scale = lax.rsqrt(jnp.mean(inputs * inputs, axis=-1, keepdims=True) + EPS)
     return inputs * scale * gain
@@ -301,9 +443,22 @@
     return masks
 
 
+def one_stretch(values, bmat, cmat, steps_dt, rate, seq_ids):
+    places = jnp.arange(values.shape[0], dtype=jnp.int32)
+    same = (places[:, None] >= places[None, :]) & (seq_ids[:, None] == seq_ids[None, :])
+    logs = jnp.cumsum(steps_dt * rate, axis=0).T
+    spans = logs[:, :, None] - logs[:, None, :]
+    factor = jnp.exp(jnp.where(same[None], spans, -1e30))
+    scores = jnp.dot(cmat, bmat.T, precision=lax.Precision.HIGH)
+    mixing = factor * scores[None] * steps_dt.T[:, None, :]
+    return jnp.einsum("htu,uhp->thp", mixing, values, precision=lax.Precision.HIGH)
+
+
 def state_space(values, bmat, cmat, steps_dt, rate, seq_ids):
     rows = values.shape[0]
     number = rows // STRETCH
+    if number == 1:
+        return one_stretch(values, bmat, cmat, steps_dt, rate, seq_ids)
     seg_blocks = seq_ids.reshape(number, STRETCH)
     before = jnp.concatenate([jnp.full((1,), -3, jnp.int32), seg_blocks[:-1, -1]])
     places = jnp.arange(STRETCH, dtype=jnp.int32)
@@ -430,9 +585,10 @@
 def per_device(tokens, cotangent, seq_ids, params, first_moment, second_moment, step_count):
     width = params.shape[0]
     rounded = params.astype(jnp.bfloat16)
-    whole = lax.all_gather(rounded, ("dp", "shard"), axis=0, tiled=True)
+    own = rounded.reshape(width // LANES, LANES)
+    whole = gather_rows(own, lax.axis_size("shard"), lax.axis_size("dp"))
     weights = unpack(whole)
-    result, grad_input, flat = block_pass(tokens, cotangent, seq_ids, weights, whole.shape[0])
+    result, grad_input, flat = block_pass(tokens, cotangent, seq_ids, weights, whole.size)
     owned = scatter_sum(flat, lax.axis_size("shard"), lax.axis_size("dp"), width // LANES)
     owned = owned.reshape(width)
     new_weight, new_first, new_second = adamw(

time: 282 us -> 197 us (0.70)
  waiting for transfers between devices: 72.5 us -> 0 us
  Pallas kernels: 72.6 us -> 128 us
  local copies, waits for them, and re-layouts: 44.6 us -> 17.5 us
  matrix products: 37.6 us -> 21.3 us
  between operations: 15.4 us -> 2.31 us
  other arithmetic: 37.7 us -> 26.9 us
    all_gather x1 -> x0, waiting for transfers between devices: 72.5 us -> none  [per_device(): whole = lax.all_gather(rounded, ('dp', 'shard'), axis=0, tiled=True)]
    pallas_call x0 -> x2, Pallas kernels: none -> 65.2 us  [the longest x1 54.8 us: gather_rows(): pl.pallas_call(functools.partial(gather_kernel, (deep, tall, wide), cuts)...]
    reshape x3 -> x1, local copies, waits for them, and re-layouts: 16 us -> 0.28 us  [unpack(): pieces.append(flat[offset:offset + length].reshape(shape))]
    dot_general x9 -> x6, matrix products: 22.4 us -> 10.2 us  [the longest x3 7.87 us: one_stretch(): jnp.einsum('htu,uhp->thp', mixing, values, precision=lax.Precision.HIGH)]
    slice x3 -> x1, local copies, waits for them, and re-layouts: 10.2 us -> 0.01 us  [unpack(): pieces.append(flat[offset:offset + length].reshape(shape))]
    pallas_call x1, Pallas kernels: 13.3 us -> 7.12 us  [pack_all(): pl.pallas_call(pack_kernel, out_shape=jax.ShapeDtypeStruct((rows, LANES),...]
    unnamed x117 -> x121, local copies, waits for them, and re-layouts: 2.21 us -> 7.25 us
    pallas_call x1, Pallas kernels: 59.3 us -> 55.8 us  [scatter_sum(): pl.pallas_call(functools.partial(scatter_kernel, (deep, tall, wide), cuts...]
  transfers between devices with their start and end apart: 1 -> 0, of which waited for: 1 -> 0; matrix products, arithmetic and copies ran while one was open for 2% -> 0% of each run, Pallas kernels for 0% -> 0%
where the time goes in v1:
time: 197 us; the launch traced here: 196 us
  Pallas kernels  128 us (65%)
  other arithmetic  26.9 us (14%)
  matrix products  21.3 us (11%)
  local copies, waits for them, and re-layouts  17.5 us (9%)
  between operations  2.31 us (1%)
    pallas_call x1, Pallas kernels, scatter_sum(): pl.pallas_call(functools.partial(scatter_kernel, (deep, tall, wide), cuts...  55.8 us
    pallas_call x1, Pallas kernels, gather_rows(): pl.pallas_call(functools.partial(gather_kernel, (deep, tall, wide), cuts)...  54.8 us
    pallas_call x1, Pallas kernels, unpack_wide(): pl.pallas_call(unpack_kernel, out_shape=(jax.ShapeDtypeStruct((D, INNER +...  10.5 us
    dot_general x3, matrix products, one_stretch(): jnp.einsum('htu,uhp->thp', mixing, values, precision=lax.Precision.HIGH)  7.87 us
    unnamed x121, local copies, waits for them, and re-layouts  7.25 us
    pallas_call x1, Pallas kernels, pack_all(): pl.pallas_call(pack_kernel, out_shape=jax.ShapeDtypeStruct((rows, LANES),...  7.12 us
    dot_general x3, matrix products, against(): lax.dot_general(left, right, (((1,), (1,)), ((), ())), preferred_element_...  6.15 us
    dot_general x3, matrix products, matmul(): return jnp.dot(left, right, preferred_element_type=jnp.float32)  4.72 us

profile of v1, /device:TPU:0, one launch (start us, length us, event | category | flops | bytes accessed | tf_op | source)
XLA Modules:
  0.0 196.2 jit_solution(2139635293697425746)
XLA Ops:
  1.4 1.0 fusion.45
  2.4 0.9 broadcast_compare_fusion
  3.4 0.8 fusion.49
  4.2 1.0 broadcast_select_fusion.cot_ref
  5.2 1.1 convert_bitcast_fusion.own
  6.3 54.8 %shard_map.118 = bf16[4,2,2,2,920,128]{5,4,3,2,1,0:T(8,128)(2,1)S(1)} custom-call(bf16[920,128]{1,0:T(8,128)(2,1)S(1)} %convert_bitcast_fusion.own), custom_call_target="tpu_custom_call" | custom-call | tf_op jit(solution)/shard_map/pallas_call | solution.py:359
  61.2 2.8 %copy-done = bf16[4,2,2,2,920,128]{5,4,3,2,1,0:T(8,128)(2,1)} copy-done((bf16[4,2,2,2,920,128]{5,4,3,2,1,0:T(8,128)(2,1)}, bf16[4,2,2,2,920,128]{5,4,3,2,1,0:T(8,128)(2,1)S(1)}, u32[]{:S(2)}) %copy-start) | copy-done | bytes 7536664
  64.1 10.5 %shard_map.119 = (bf16[768,3328]{1,0:T(8,128)(2,1)}, bf16[1536,768]{1,0:T(8,128)(2,1)S(1)}) custom-call(bf16[29440,128]{1,0:T(8,128)(2,1)} %bitcast.94), custom_call_target="tpu_custom_call" | custom-call | tf_op jit(solution)/shard_map/pallas_call | solution.py:416
  74.5 0.1 fusion.73
  74.6 0.1 slice_convert_fusion.2
  74.7 0.1 slice_convert_fusion.1
  74.8 0.3 reshape.233
  75.1 0.1 fusion.42.normed_ref
  75.2 0.2 compare_select_fusion.2
  75.4 0.1 fusion.64
  75.5 0.1 copy.49
  75.6 0.2 reduce_window_sum.22
  75.8 3.3 %fusion.83 = f32[128,3328]{1,0:T(8,128)S(1)} fusion(bf16[128,768]{1,0:T(8,128)(2,1)S(1)} %fusion.42.normed_ref, bf16[768,3328]{1,0:T(8,128)(2,1)} %get-tuple-element.8), kind=kOutput, calls=%fused_computation.144 | convolution fusion | flops 654311424 | bytes 7012352 | tf_op jit(solution)/shard_map/dot_general | solution.py:35
  79.2 0.1 slice.119
  79.3 0.1 slice.115
  79.5 0.9 copy-done.1
  80.4 0.3 copy-done.7
  80.7 1.6 fusion.23
  82.3 0.2 fusion.52
  82.5 0.7 copy-done.9
  83.3 1.0 slice.120
  84.2 2.3 %copy.48 = f32[128,1536]{0,1:T(8,128)} copy(f32[128,1536]{1,0:T(8,128)} %slice.120) | data formatting | bytes 1572864 | tf_op jit(solution)/shard_map/jvp()/slice | solution.py:515
  86.6 4.0 %fusion.15 = f32[128,24,64]{0,2,1:T(8,128)} fusion(f32[128,24,64]{0,2,1:T(8,128)} %bitcast.98, f32[24,128]{1,0:T(8,128)S(1)} %get-tuple-element.54, f32[128,128]{1,0:T(8,128)S(1)} %fusion.52, f32[24,128]{1,0:T(8,128)S(1)} %copy.50, pred[128,128]{1,0:T(8,128)(4,1)S(1)} %fusion.49, f32[24]{0:T(128)S(1)} %get-tuple-element.43), kind=kOutput, calls=%fused_computation.13 | convolution fusion | flops 152961024 | bytes 1679456 | tf_op jit(solution)/shard_map/jvp(htu,uhp->thp)/dot_general | solution.py:454
  90.6 2.3 %copy.52 = f32[128,1536]{1,0:T(8,128)} copy(f32[128,1536]{0,1:T(8,128)} %bitcast.104) | data formatting | bytes 1572864 | tf_op jit(solution)/shard_map/jvp()/reshape | solution.py:521
  92.9 1.7 multiply_reduce_fusion.9
  94.7 1.5 multiply_reduce_fusion.6
  96.2 3.6 %multiply_reduce_fusion.7 = (f32[1536]{0:T(1024)}, f32[128,1536]{1,0:T(8,128)}, f32[128,1536]{1,0:T(8,128)}, bf16[128,1536]{1,0:T(8,128)(2,1)S(1)}) fusion(f32[128,1792]{1,0:T(8,128)S(1)} %copy-done.10, f32[128,3328]{1,0:T(8,128)} %copy-done.1, f32[128,1536]{1,0:T(8,128)S(1)} %get-tuple-element.35, f32[128]{0:T(128)S(1)} %multiply_multiply_fusion.2, ...), kind=kLoop, calls=%fused_computation.38 | loop fusion | flops 4323840 | bytes 5911552 | tf_op jit(solution)/shard_map/transpose(jvp())/reduce_sum | solution.py:520
  99.9 1.2 fusion.18
  101.0 0.8 reduce_sum.198
  101.9 0.6 reduce_sum.202
  102.5 1.4 copy.53
  103.9 2.8 %fusion.20 = (f32[24,128]{1,0:T(8,128)S(1)}, f32[24,128]{1,0:T(8,128)S(1)}, f32[24,128]{1,0:T(8,128)S(1)}, f32[128,128]{1,0:T(8,128)S(1)}) fusion(f32[24,128]{1,0:T(8,128)S(1)} %copy-done.38, f32[128,128]{1,0:T(8,128)S(1)} %copy-done.31, f32[24,128]{1,0:T(8,128)S(1)} %copy-done.40, pred[128,128]{1,0:T(8,128)(4,1)S(1)} %copy-done.36, ...), kind=kOutput, calls=%fused_computation.21 | convolution fusion | flops 156081152 | bytes 1781760 | tf_op jit(solution)/shard_map/transpose(jvp(htu,uhp->thp))/dot_general | solution.py:454
  106.7 1.1 fusion.12
  107.9 1.2 copy.54
  109.1 0.1 copy.56
  109.2 1.1 reduce_window_sum.23
  110.4 0.7 fusion.79
  111.1 1.3 negate_multiply_fusion
  112.4 1.1 fusion.54
  113.5 1.0 fusion.50
  114.5 2.9 %multiply_reduce_fusion.5 = (f32[1792]{0:T(1024)S(1)}, f32[128,1792]{1,0:T(8,128)}, f32[128,1792]{1,0:T(8,128)S(1)}) fusion(f32[125,1792]{1,0:T(8,128)S(1)} %copy-done.8, f32[128]{0:T(128)S(1)} %copy-done.50, f32[128,1792]{1,0:T(8,128)} %get-tuple-element.37, f32[128,1536]{1,0:T(8,128)} %copy.54, f32[128,128]{1,0:T(8,128)S(1)} %fusion.54, ...), kind=kLoop, calls=%fused_computation.30 | loop fusion | flops 3209472 | bytes 4573696 | tf_op jit(solution)/shard_map/transpose(jvp())/reduce_sum | solution.py:513
  117.5 1.4 multiply_reduce_fusion.4
  119.0 0.2 fusion.66
  119.2 0.2 reshape.239
  119.5 1.4 slice_multiply_fusion.1
  120.9 0.1 slice_multiply_fusion
  121.0 0.1 slice_multiply_fusion.2
  121.1 1.2 copy-done.2
  122.3 0.4 fusion.76
  122.8 0.2 copy-done.34
  123.0 0.1 concatenate.19
  123.1 1.2 add_convert_fusion.proj_ref
  124.4 4.2 %fusion.84 = f32[128,768]{1,0:T(8,128)S(1)} fusion(bf16[128,3328]{1,0:T(8,128)(2,1)S(1)} %add_convert_fusion.proj_ref, bf16[768,3328]{1,0:T(8,128)(2,1)} %get-tuple-element.8), kind=kOutput, calls=%fused_computation.145 | convolution fusion | flops 654311424 | bytes 6356992 | tf_op jit(solution)/shard_map/dot_general | solution.py:45
  128.7 0.4 fusion.43
  129.1 0.9 fusion.44
  130.0 7.1 %shard_map.120 = bf16[29440,128]{1,0:T(8,128)(2,1)} custom-call(f32[6,128]{1,0:T(8,128)S(1)} %bitcast.95, f32[227,128]{1,0:T(8,128)S(1)} %pad_bitcast_fusion.small_ref, bf16[128,768]{1,0:T(8,128)(2,1)S(1)} %fusion.42.normed_ref, bf16[128,3328]{1,0:T(8,128)(2,1)S(1)} %add_convert_fusion.proj_ref, bf16[128,1536]{1,0:T(8,128)(2,1)S(1)} %get-tuple-element.42.hidden_ref, ...), custom_call_target="tpu_custom_call" | custom-call | tf_op jit(solution)/shard_map/pallas_call | solution.py:114
  137.1 55.8 %shard_map.121 = f32[920,128]{1,0:T(8,128)} custom-call(bf16[4,2,2,2,920,128]{5,4,3,2,1,0:T(8,128)(2,1)} %bitcast.96), custom_call_target="tpu_custom_call" | custom-call | tf_op jit(solution)/shard_map/pallas_call | solution.py:264
  193.0 2.4 %multiply_subtract_fusion = (f32[117760]{0:T(1024)}, f32[117760]{0:T(1024)}, f32[117760]{0:T(1024)}) fusion(f32[117760]{0:T(1024)S(1)} %copy-done.15, f32[]{:T(128)} %bitcast.26, f32[]{:T(128)} %bitcast.25, f32[117760]{0:T(1024)S(1)} %copy-done.18, f32[117760]{0:T(1024)S(1)} %copy-done.19, f32[920,128]{1,0:T(8,128)} %shard_map.121), kind=kLoop, calls=%fused_computation.63 | loop fusion | flops 1766400 | bytes 3297288 | tf_op jit(solution)/shard_map/sub | solution.py:579
  195.4 0.8 copy.63
  (135 shorter events, 0.6 us)
Async XLA Ops:
  2.4 0.9 copy-start.55
  2.4 72.6 %copy-start.41 = (f32[128]{0:T(128)}, f32[128]{0:T(128)S(1)}, u32[]{:S(2)}) copy-start(f32[128]{0:T(128)S(1)} %fusion.71) | copy-start | bytes 1540
  3.3 57.7 %copy-start.43 = (pred[128]{0:T(512)(128)(4,1)}, pred[128]{0:T(512)(128)(4,1)S(1)}, u32[]{:S(2)}) copy-start(pred[128]{0:T(512)(128)(4,1)S(1)} %get-tuple-element.50) | copy-start | bytes 388
  3.3 76.1 %copy-start.45 = (f32[128]{0:T(128)}, f32[128]{0:T(128)S(1)}, u32[]{:S(2)}) copy-start(f32[128]{0:T(128)S(1)} %get-tuple-element.51) | copy-start | bytes 1540
  3.3 76.1 %copy-start.47 = (f32[128]{0:T(128)}, f32[128]{0:T(128)S(1)}, u32[]{:S(2)}) copy-start(f32[128]{0:T(128)S(1)} %get-tuple-element.52) | copy-start | bytes 1540
  3.3 76.1 %copy-start.49 = (f32[128]{0:T(128)}, f32[128]{0:T(128)S(1)}, u32[]{:S(2)}) copy-start(f32[128]{0:T(128)S(1)} %get-tuple-element.53) | copy-start | bytes 1540
  4.2 82.4 %copy-start.35 = (pred[128,128]{1,0:T(8,128)(4,1)}, pred[128,128]{1,0:T(8,128)(4,1)S(1)}, u32[]{:S(2)}) copy-start(pred[128,128]{1,0:T(8,128)(4,1)S(1)} %fusion.49) | copy-start | bytes 49156
  61.1 3.0 %copy-start = (bf16[4,2,2,2,920,128]{5,4,3,2,1,0:T(8,128)(2,1)}, bf16[4,2,2,2,920,128]{5,4,3,2,1,0:T(8,128)(2,1)S(1)}, u32[]{:S(2)}) copy-start(bf16[4,2,2,2,920,128]{5,4,3,2,1,0:T(8,128)(2,1)S(1)} %shard_map.118) | copy-start | bytes 22609924
  61.1 18.3 %copy-start.21 = (f32[1792]{0:T(1024)}, f32[1792]{0:T(1024)S(1)}, u32[]{:S(2)}) copy-start(f32[1792]{0:T(1024)S(1)} %get-tuple-element.45) | copy-start | bytes 21508
  61.1 18.3 %copy-start.23 = (f32[1792]{0:T(1024)}, f32[1792]{0:T(1024)S(1)}, u32[]{:S(2)}) copy-start(f32[1792]{0:T(1024)S(1)} %get-tuple-element.46) | copy-start | bytes 21508
  61.1 18.3 %copy-start.25 = (f32[1792]{0:T(1024)}, f32[1792]{0:T(1024)S(1)}, u32[]{:S(2)}) copy-start(f32[1792]{0:T(1024)S(1)} %get-tuple-element.48) | copy-start | bytes 21508
  61.2 18.3 %copy-start.27 = (f32[1792]{0:T(1024)}, f32[1792]{0:T(1024)S(1)}, u32[]{:S(2)}) copy-start(f32[1792]{0:T(1024)S(1)} %get-tuple-element.47) | copy-start | bytes 21508
  64.1 10.6 %copy-start.29 = (bf16[29056]{0:T(1024)(128)(2,1)}, bf16[29056]{0:T(1024)(128)(2,1)S(1)}, u32[]{:S(2)}) copy-start(bf16[29056]{0:T(1024)(128)(2,1)S(1)} %slice_bitcast_fusion) | copy-start | bytes 174340
  64.1 11.0 %copy-start.12 = (bf16[128,768]{1,0:T(8,128)(2,1)S(1)}, bf16[128,768]{1,0:T(8,128)(2,1)}, u32[]{:S(2)}) copy-start(bf16[128,768]{1,0:T(8,128)(2,1)} %param.7) | copy-start | bytes 589828
  74.6 4.6 %copy-start.52 = (f32[24]{0:T(128)}, f32[24]{0:T(128)S(1)}, u32[]{:S(2)}) copy-start(f32[24]{0:T(128)S(1)} %fusion.73) | copy-start | bytes 292
  74.7 11.9 %copy-start.58 = (f32[24]{0:T(128)}, f32[24]{0:T(128)S(1)}, u32[]{:S(2)}) copy-start(f32[24]{0:T(128)S(1)} %get-tuple-element.43) | copy-start | bytes 292
  74.7 19.9 %copy-start.20 = (f32[1536]{0:T(1024)}, f32[1536]{0:T(1024)S(1)}, u32[]{:S(2)}) copy-start(f32[1536]{0:T(1024)S(1)} %slice_convert_fusion.1) | copy-start | bytes 18436
  75.4 11.2 %copy-start.37 = (f32[24,128]{1,0:T(8,128)}, f32[24,128]{1,0:T(8,128)S(1)}, u32[]{:S(2)}) copy-start(f32[24,128]{1,0:T(8,128)S(1)} %get-tuple-element.54) | copy-start | bytes 36868
  75.8 10.8 %copy-start.39 = (f32[24,128]{1,0:T(8,128)}, f32[24,128]{1,0:T(8,128)S(1)}, u32[]{:S(2)}) copy-start(f32[24,128]{1,0:T(8,128)S(1)} %copy.50) | copy-start | bytes 36868
  79.2 1.2 copy-start.1
  79.3 1.4 copy-start.7
  79.3 3.0 %copy-start.3 = (f32[126,1792]{1,0:T(8,128)}, f32[126,1792]{1,0:T(8,128)S(1)}, u32[]{:S(2)}) copy-start(f32[126,1792]{1,0:T(8,128)S(1)} %slice.117) | copy-start | bytes 2709508
  80.7 1.6 copy-start.5
  82.3 0.9 copy-start.9
  83.3 3.4 %copy-start.30 = (f32[128,128]{1,0:T(8,128)}, f32[128,128]{1,0:T(8,128)S(1)}, u32[]{:S(2)}) copy-start(f32[128,128]{1,0:T(8,128)S(1)} %fusion.52) | copy-start | bytes 196612
  94.6 1.6 copy-start.10
  94.6 1.6 copy-start.11
  101.0 2.9 %copy-start.17 = (f32[128,1536]{0,1:T(8,128)S(1)}, f32[128,1536]{0,1:T(8,128)}, u32[]{:S(2)}) copy-start(f32[128,1536]{0,1:T(8,128)} %copy.48) | copy-start | bytes 2359300
  101.0 2.9 %copy-start.31 = (f32[128,128]{1,0:T(8,128)S(1)}, f32[128,128]{1,0:T(8,128)}, u32[]{:S(2)}) copy-start(f32[128,128]{1,0:T(8,128)} %copy-done.30) | copy-start | bytes 196612
  101.0 2.9 %copy-start.36 = (pred[128,128]{1,0:T(8,128)(4,1)S(1)}, pred[128,128]{1,0:T(8,128)(4,1)}, u32[]{:S(2)}) copy-start(pred[128,128]{1,0:T(8,128)(4,1)} %copy-done.35) | copy-start | bytes 49156
  101.0 2.9 %copy-start.38 = (f32[24,128]{1,0:T(8,128)S(1)}, f32[24,128]{1,0:T(8,128)}, u32[]{:S(2)}) copy-start(f32[24,128]{1,0:T(8,128)} %copy-done.37) | copy-start | bytes 36868
  101.0 2.9 %copy-start.40 = (f32[24,128]{1,0:T(8,128)S(1)}, f32[24,128]{1,0:T(8,128)}, u32[]{:S(2)}) copy-start(f32[24,128]{1,0:T(8,128)} %copy-done.39) | copy-start | bytes 36868
  103.9 2.8 %copy-start.59 = (f32[24]{0:T(128)S(1)}, f32[24]{0:T(128)}, u32[]{:S(2)}) copy-start(f32[24]{0:T(128)} %copy-done.58) | copy-start | bytes 292
  107.9 2.5 %copy-start.53 = (f32[24]{0:T(128)S(1)}, f32[24]{0:T(128)}, u32[]{:S(2)}) copy-start(f32[24]{0:T(128)} %copy-done.52) | copy-start | bytes 292
  107.9 6.6 %copy-start.8 = (f32[125,1792]{1,0:T(8,128)S(1)}, f32[125,1792]{1,0:T(8,128)}, u32[]{:S(2)}) copy-start(f32[125,1792]{1,0:T(8,128)} %copy-done.7) | copy-start | bytes 2688004
  107.9 6.6 %copy-start.50 = (f32[128]{0:T(128)S(1)}, f32[128]{0:T(128)}, u32[]{:S(2)}) copy-start(f32[128]{0:T(128)} %copy-done.49) | copy-start | bytes 1540
  111.1 7.9 %copy-start.32 = (bf16[128,24]{0,1:T(8,128)(2,1)}, bf16[128,24]{0,1:T(8,128)(2,1)S(1)}, u32[]{:S(2)}) copy-start(bf16[128,24]{0,1:T(8,128)(2,1)S(1)} %get-tuple-element.26) | copy-start | bytes 18436
  114.5 3.0 %copy-start.4 = (f32[126,1792]{1,0:T(8,128)S(1)}, f32[126,1792]{1,0:T(8,128)}, u32[]{:S(2)}) copy-start(f32[126,1792]{1,0:T(8,128)} %copy-done.3) | copy-start | bytes 2709508
  114.5 3.0 %copy-start.6 = (f32[127,1792]{1,0:T(8,128)S(1)}, f32[127,1792]{1,0:T(8,128)}, u32[]{:S(2)}) copy-start(f32[127,1792]{1,0:T(8,128)} %copy-done.5) | copy-start | bytes 2731012
  114.5 3.0 %copy-start.46 = (f32[128]{0:T(128)S(1)}, f32[128]{0:T(128)}, u32[]{:S(2)}) copy-start(f32[128]{0:T(128)} %copy-done.45) | copy-start | bytes 1540
  114.5 3.0 %copy-start.48 = (f32[128]{0:T(128)S(1)}, f32[128]{0:T(128)}, u32[]{:S(2)}) copy-start(f32[128]{0:T(128)} %copy-done.47) | copy-start | bytes 1540
  117.5 1.9 copy-start.28
  118.9 1.9 copy-start.26
  119.4 1.5 copy-start.14
  119.5 1.5 copy-start.24
  120.8 1.5 copy-start.2
  120.8 1.5 copy-start.22
  122.3 0.7 copy-start.34
  122.3 0.7 copy-start.51
  122.3 0.7 copy-start.54
  122.3 0.7 copy-start.57
  124.3 4.3 %copy-start.33 = (bf16[128,24]{0,1:T(8,128)(2,1)S(1)}, bf16[128,24]{0,1:T(8,128)(2,1)}, u32[]{:S(2)}) copy-start(bf16[128,24]{0,1:T(8,128)(2,1)} %copy-done.32) | copy-start | bytes 18436
  124.3 4.3 %copy-start.42 = (f32[128]{0:T(128)S(1)}, f32[128]{0:T(128)}, u32[]{:S(2)}) copy-start(f32[128]{0:T(128)} %copy-done.41) | copy-start | bytes 1540
  124.4 4.7 %copy-start.56 = (f32[128]{0:T(128)S(1)}, f32[128]{0:T(128)}, u32[]{:S(2)}) copy-start(f32[128]{0:T(128)} %copy-done.55) | copy-start | bytes 1540
  124.4 4.7 %copy-start.16 = (bf16[128,768]{1,0:T(8,128)(2,1)S(1)}, bf16[128,768]{1,0:T(8,128)(2,1)}, u32[]{:S(2)}) copy-start(bf16[128,768]{1,0:T(8,128)(2,1)} %param.8) | copy-start | bytes 589828
  124.4 4.7 %copy-start.44 = (pred[128]{0:T(512)(128)(4,1)S(1)}, pred[128]{0:T(512)(128)(4,1)}, u32[]{:S(2)}) copy-start(pred[128]{0:T(512)(128)(4,1)} %copy-done.43) | copy-start | bytes 388
  137.1 55.8 %copy-start.15 = (f32[117760]{0:T(1024)S(1)}, f32[117760]{0:T(1024)}, u32[]{:S(2)}) copy-start(f32[117760]{0:T(1024)} %param.10) | copy-start | bytes 1413124
  137.1 55.8 %copy-start.18 = (f32[117760]{0:T(1024)S(1)}, f32[117760]{0:T(1024)}, u32[]{:S(2)}) copy-start(f32[117760]{0:T(1024)} %param.12) | copy-start | bytes 1413124
  137.1 55.8 %copy-start.19 = (f32[117760]{0:T(1024)S(1)}, f32[117760]{0:T(1024)}, u32[]{:S(2)}) copy-start(f32[117760]{0:T(1024)} %param.11) | copy-start | bytes 1413124
  193.0 2.4 %copy-start.13 = (f32[920,128]{1,0:T(8,128)S(1)}, f32[920,128]{1,0:T(8,128)}, u32[]{:S(2)}) copy-start(f32[920,128]{1,0:T(8,128)} %shard_map.121) | copy-start | bytes 1413124

commit v2 on v1

--- a/solution.py
+++ b/solution.py
@@ -18,6 +18,7 @@
 CHANNELS = 1792
 LANES = 128
 CUTS = 8
+LAG = 2
 SPAN = 256
 MESH = pl.DeviceIdType.MESH
 PACKED = D + D * (INNER + CHANNELS) + D * HEADS + (KERNEL + 1) * CHANNELS + 3 * HEADS + INNER + INNER * D
@@ -124,6 +125,13 @@
     )(gain, small, normed, proj, hidden, cot)
 
 
+def in_waves(stages, count):
+    for wave in range(count + LAG * (len(stages) - 1)):
+        for number, stage in enumerate(stages):
+            if 0 <= wave - LAG * number < count:
+                stage(wave - LAG * number)
+
+
 def scatter_kernel(grid, cuts, data, out, send_sem, recv_sem, *refs):
     deep, tall, wide = grid
     dp, shard = lax.axis_index("dp"), lax.axis_index("shard")
@@ -173,7 +181,8 @@
     for k, (start, size) in enumerate(cuts):
         src = data.at[:, :, :, 1 - c, start : start + size]
         flights.append([push(k, 0, src, chunks[k][0], partner)])
-    for k, (start, size) in enumerate(cuts):
+    def stage_one(k):
+        start, size = cuts[k]
         got, acc, got_one = chunks[k][:3]
         for copy in flights[k]:
             copy.wait_recv()
@@ -193,7 +202,8 @@
         else:
             for j, p in enumerate(ys):
                 flights[k].append(push(k, first_y + j, acc.at[:, p], got_one.at[j], to_y[j]))
-    for k, (start, size) in enumerate(cuts):
+    def stage_two(k):
+        start, size = cuts[k]
         got, acc, got_one, acc_two, got_two = chunks[k][:5]
         for copy in flights[k]:
             copy.wait_recv()
@@ -214,7 +224,8 @@
         else:
             for j, p in enumerate(xs):
                 flights[k].append(push(k, first_x + j, acc_two.at[:, p], got_two.at[j], to_x[j]))
-    for k, (start, size) in enumerate(cuts):
+    def stage_three(k):
+        start, size = cuts[k]
         acc_two, got_two, acc_three, got_three = chunks[k][3:]
         for copy in flights[k]:
             copy.wait_recv()
@@ -229,12 +240,15 @@
         flights[k] = []
         for j, p in enumerate(zs):
             flights[k].append(push(k, first_z + j, acc_three.at[p], got_three.at[j], to_z[j]))
-    for k, (start, size) in enumerate(cuts):
+    def stage_four(k):
+        start, size = cuts[k]
         acc_three, got_three = chunks[k][5:]
         for copy in flights[k]:
             copy.wait_recv()
         parts = [acc_three[z]] + [got_three[j] for j in range(deep - 1)]
         out[start : start + size, :] = total(parts)
+
+    in_waves((stage_one, stage_two, stage_three, stage_four), len(cuts))
     for copy in sent:
         copy.wait_send()
 
@@ -316,7 +330,8 @@
         rows = pl.ds(start, size)
         flights.append(push(k, first_z, own.at[rows], out.at[z, y, x, c, rows], to_z))
     out[z, y, x, c] = own[...]
-    for k, (start, size) in enumerate(cuts):
+    def stage_one(k):
+        start, size = cuts[k]
         rows = pl.ds(start, size)
         for copy in flights[k]:
             copy.wait_recv()
@@ -325,7 +340,8 @@
             flights[k] = push(k, first_y, line, line, to_y)
         else:
             flights[k] = push(k, first_x, line, line, to_x)
-    for k, (start, size) in enumerate(cuts):
+    def stage_two(k):
+        start, size = cuts[k]
         rows = pl.ds(start, size)
         for copy in flights[k]:
             copy.wait_recv()
@@ -335,11 +351,13 @@
         else:
             sheet = out.at[:, y, :, c, rows]
             flights[k] = push(k, first_y, sheet, sheet, to_y)
-    for k, (start, size) in enumerate(cuts):
+    def stage_three(k):
+        start, size = cuts[k]
         for copy in flights[k]:
             copy.wait_recv()
         cube = out.at[:, :, :, c, pl.ds(start, size)]
         flights[k] = push(k, 0, cube, cube, [partner])
+    in_waves((stage_one, stage_two, stage_three), len(cuts))
     for flight in flights:
         for copy in flight:
             copy.wait_recv()

time: 197 us -> 187 us (0.949)
  Pallas kernels: 128 us -> 118 us
    pallas_call x1, Pallas kernels: 55.8 us -> 50.4 us  [scatter_sum(): pl.pallas_call(functools.partial(scatter_kernel, (deep, tall, wide), cuts...]
    pallas_call x1, Pallas kernels: 54.8 us -> 49.9 us  [gather_rows(): pl.pallas_call(functools.partial(gather_kernel, (deep, tall, wide), cuts)...]
where the time goes in v2:
time: 187 us; the launch traced here: 186 us
  Pallas kernels  118 us (63%)
  other arithmetic  26.9 us (14%)
  matrix products  21.3 us (11%)
  local copies, waits for them, and re-layouts  17.5 us (9%)
  between operations  2.31 us (1%)
    pallas_call x1, Pallas kernels, scatter_sum(): pl.pallas_call(functools.partial(scatter_kernel, (deep, tall, wide), cuts...  50.4 us
    pallas_call x1, Pallas kernels, gather_rows(): pl.pallas_call(functools.partial(gather_kernel, (deep, tall, wide), cuts)...  49.9 us
    pallas_call x1, Pallas kernels, unpack_wide(): pl.pallas_call(unpack_kernel, out_shape=(jax.ShapeDtypeStruct((D, INNER +...  10.5 us
    dot_general x3, matrix products, one_stretch(): jnp.einsum('htu,uhp->thp', mixing, values, precision=lax.Precision.HIGH)  7.86 us
    unnamed x121, local copies, waits for them, and re-layouts  7.25 us
    pallas_call x1, Pallas kernels, pack_all(): pl.pallas_call(pack_kernel, out_shape=jax.ShapeDtypeStruct((rows, LANES),...  7.12 us
    dot_general x3, matrix products, against(): lax.dot_general(left, right, (((1,), (1,)), ((), ())), preferred_element_...  6.15 us
    dot_general x3, matrix products, matmul(): return jnp.dot(left, right, preferred_element_type=jnp.float32)  4.72 us

profile of v2, /device:TPU:0, one launch (start us, length us, event | category | flops | bytes accessed | tf_op | source)
XLA Modules:
  0.0 185.8 jit_solution(12210832062291073154)
XLA Ops:
  1.4 1.0 fusion.45
  2.4 0.9 broadcast_compare_fusion
  3.4 0.8 fusion.49
  4.2 1.0 broadcast_select_fusion.cot_ref
  5.2 1.1 convert_bitcast_fusion.own
  6.3 49.9 %shard_map.118 = bf16[4,2,2,2,920,128]{5,4,3,2,1,0:T(8,128)(2,1)S(1)} custom-call(bf16[920,128]{1,0:T(8,128)(2,1)S(1)} %convert_bitcast_fusion.own), custom_call_target="tpu_custom_call" | custom-call | tf_op jit(solution)/shard_map/pallas_call | solution.py:377
  56.3 2.8 %copy-done = bf16[4,2,2,2,920,128]{5,4,3,2,1,0:T(8,128)(2,1)} copy-done((bf16[4,2,2,2,920,128]{5,4,3,2,1,0:T(8,128)(2,1)}, bf16[4,2,2,2,920,128]{5,4,3,2,1,0:T(8,128)(2,1)S(1)}, u32[]{:S(2)}) %copy-start) | copy-done | bytes 7536664
  59.1 10.5 %shard_map.119 = (bf16[768,3328]{1,0:T(8,128)(2,1)}, bf16[1536,768]{1,0:T(8,128)(2,1)S(1)}) custom-call(bf16[29440,128]{1,0:T(8,128)(2,1)} %bitcast.94), custom_call_target="tpu_custom_call" | custom-call | tf_op jit(solution)/shard_map/pallas_call | solution.py:434
  69.6 0.1 fusion.73
  69.7 0.1 slice_convert_fusion.2
  69.7 0.1 slice_convert_fusion.1
  69.8 0.3 reshape.233
  70.1 0.1 fusion.42.normed_ref
  70.2 0.2 compare_select_fusion.2
  70.5 0.1 fusion.64
  70.6 0.1 copy.49
  70.7 0.2 reduce_window_sum.22
  70.9 3.3 %fusion.83 = f32[128,3328]{1,0:T(8,128)S(1)} fusion(bf16[128,768]{1,0:T(8,128)(2,1)S(1)} %fusion.42.normed_ref, bf16[768,3328]{1,0:T(8,128)(2,1)} %get-tuple-element.8), kind=kOutput, calls=%fused_computation.144 | convolution fusion | flops 654311424 | bytes 7012352 | tf_op jit(solution)/shard_map/dot_general | solution.py:36
  74.3 0.1 slice.119
  74.4 0.1 slice.115
  74.6 0.9 copy-done.1
  75.5 0.3 copy-done.7
  75.8 1.6 fusion.23
  77.4 0.2 fusion.52
  77.6 0.7 copy-done.9
  78.3 1.0 slice.120
  79.3 2.3 %copy.48 = f32[128,1536]{0,1:T(8,128)} copy(f32[128,1536]{1,0:T(8,128)} %slice.120) | data formatting | bytes 1572864 | tf_op jit(solution)/shard_map/jvp()/slice | solution.py:533
  81.7 4.0 %fusion.15 = f32[128,24,64]{0,2,1:T(8,128)} fusion(f32[128,24,64]{0,2,1:T(8,128)} %bitcast.98, f32[24,128]{1,0:T(8,128)S(1)} %get-tuple-element.54, f32[128,128]{1,0:T(8,128)S(1)} %fusion.52, f32[24,128]{1,0:T(8,128)S(1)} %copy.50, pred[128,128]{1,0:T(8,128)(4,1)S(1)} %fusion.49, f32[24]{0:T(128)S(1)} %get-tuple-element.43), kind=kOutput, calls=%fused_computation.13 | convolution fusion | flops 152961024 | bytes 1679456 | tf_op jit(solution)/shard_map/jvp(htu,uhp->thp)/dot_general | solution.py:472
  85.7 2.3 %copy.52 = f32[128,1536]{1,0:T(8,128)} copy(f32[128,1536]{0,1:T(8,128)} %bitcast.104) | data formatting | bytes 1572864 | tf_op jit(solution)/shard_map/jvp()/reshape | solution.py:539
  88.0 1.7 multiply_reduce_fusion.9
  89.7 1.5 multiply_reduce_fusion.6
  91.3 3.6 %multiply_reduce_fusion.7 = (f32[1536]{0:T(1024)}, f32[128,1536]{1,0:T(8,128)}, f32[128,1536]{1,0:T(8,128)}, bf16[128,1536]{1,0:T(8,128)(2,1)S(1)}) fusion(f32[128,1792]{1,0:T(8,128)S(1)} %copy-done.10, f32[128,3328]{1,0:T(8,128)} %copy-done.1, f32[128,1536]{1,0:T(8,128)S(1)} %get-tuple-element.35, f32[128]{0:T(128)S(1)} %multiply_multiply_fusion.2, ...), kind=kLoop, calls=%fused_computation.38 | loop fusion | flops 4323840 | bytes 5911552 | tf_op jit(solution)/shard_map/transpose(jvp())/reduce_sum | solution.py:538
  94.9 1.2 fusion.18
  96.1 0.8 reduce_sum.198
  96.9 0.6 reduce_sum.202
  97.5 1.4 copy.53
  99.0 2.8 %fusion.20 = (f32[24,128]{1,0:T(8,128)S(1)}, f32[24,128]{1,0:T(8,128)S(1)}, f32[24,128]{1,0:T(8,128)S(1)}, f32[128,128]{1,0:T(8,128)S(1)}) fusion(f32[24,128]{1,0:T(8,128)S(1)} %copy-done.38, f32[128,128]{1,0:T(8,128)S(1)} %copy-done.31, f32[24,128]{1,0:T(8,128)S(1)} %copy-done.40, pred[128,128]{1,0:T(8,128)(4,1)S(1)} %copy-done.36, ...), kind=kOutput, calls=%fused_computation.21 | convolution fusion | flops 156081152 | bytes 1781760 | tf_op jit(solution)/shard_map/transpose(jvp(htu,uhp->thp))/dot_general | solution.py:472
  101.8 1.1 fusion.12
  103.0 1.2 copy.54
  104.2 0.1 copy.56
  104.3 1.1 reduce_window_sum.23
  105.4 0.7 fusion.79
  106.2 1.3 negate_multiply_fusion
  107.4 1.1 fusion.54
  108.5 1.0 fusion.50
  109.6 2.9 %multiply_reduce_fusion.5 = (f32[1792]{0:T(1024)S(1)}, f32[128,1792]{1,0:T(8,128)}, f32[128,1792]{1,0:T(8,128)S(1)}) fusion(f32[125,1792]{1,0:T(8,128)S(1)} %copy-done.8, f32[128]{0:T(128)S(1)} %copy-done.50, f32[128,1792]{1,0:T(8,128)} %get-tuple-element.37, f32[128,1536]{1,0:T(8,128)} %copy.54, f32[128,128]{1,0:T(8,128)S(1)} %fusion.54, ...), kind=kLoop, calls=%fused_computation.30 | loop fusion | flops 3209472 | bytes 4573696 | tf_op jit(solution)/shard_map/transpose(jvp())/reduce_sum | solution.py:531
  112.6 1.4 multiply_reduce_fusion.4
  114.0 0.2 fusion.66
  114.3 0.2 reshape.239
  114.5 1.4 slice_multiply_fusion.1
  115.9 0.1 slice_multiply_fusion
  116.0 0.1 slice_multiply_fusion.2
  116.1 1.2 copy-done.2
  117.4 0.4 fusion.76
  117.9 0.2 copy-done.34
  118.1 0.1 concatenate.19
  118.2 1.2 add_convert_fusion.proj_ref
  119.5 4.2 %fusion.84 = f32[128,768]{1,0:T(8,128)S(1)} fusion(bf16[128,3328]{1,0:T(8,128)(2,1)S(1)} %add_convert_fusion.proj_ref, bf16[768,3328]{1,0:T(8,128)(2,1)} %get-tuple-element.8), kind=kOutput, calls=%fused_computation.145 | convolution fusion | flops 654311424 | bytes 6356992 | tf_op jit(solution)/shard_map/dot_general | solution.py:46
  123.7 0.4 fusion.43
  124.1 0.9 fusion.44
  125.1 7.1 %shard_map.120 = bf16[29440,128]{1,0:T(8,128)(2,1)} custom-call(f32[6,128]{1,0:T(8,128)S(1)} %bitcast.95, f32[227,128]{1,0:T(8,128)S(1)} %pad_bitcast_fusion.small_ref, bf16[128,768]{1,0:T(8,128)(2,1)S(1)} %fusion.42.normed_ref, bf16[128,3328]{1,0:T(8,128)(2,1)S(1)} %add_convert_fusion.proj_ref, bf16[128,1536]{1,0:T(8,128)(2,1)S(1)} %get-tuple-element.42.hidden_ref, ...), custom_call_target="tpu_custom_call" | custom-call | tf_op jit(solution)/shard_map/pallas_call | solution.py:115
  132.2 50.4 %shard_map.121 = f32[920,128]{1,0:T(8,128)} custom-call(bf16[4,2,2,2,920,128]{5,4,3,2,1,0:T(8,128)(2,1)} %bitcast.96), custom_call_target="tpu_custom_call" | custom-call | tf_op jit(solution)/shard_map/pallas_call | solution.py:278
  182.7 2.4 %multiply_subtract_fusion = (f32[117760]{0:T(1024)}, f32[117760]{0:T(1024)}, f32[117760]{0:T(1024)}) fusion(f32[117760]{0:T(1024)S(1)} %copy-done.15, f32[]{:T(128)} %bitcast.26, f32[]{:T(128)} %bitcast.25, f32[117760]{0:T(1024)S(1)} %copy-done.18, f32[117760]{0:T(1024)S(1)} %copy-done.19, f32[920,128]{1,0:T(8,128)} %shard_map.121), kind=kLoop, calls=%fused_computation.63 | loop fusion | flops 1766400 | bytes 3297288 | tf_op jit(solution)/shard_map/sub | solution.py:597
  185.0 0.8 copy.63
  (135 shorter events, 0.6 us)
Async XLA Ops:
  2.4 0.9 copy-start.55
  2.4 67.7 %copy-start.41 = (f32[128]{0:T(128)}, f32[128]{0:T(128)S(1)}, u32[]{:S(2)}) copy-start(f32[128]{0:T(128)S(1)} %fusion.71) | copy-start | bytes 1540
  3.3 52.8 %copy-start.43 = (pred[128]{0:T(512)(128)(4,1)}, pred[128]{0:T(512)(128)(4,1)S(1)}, u32[]{:S(2)}) copy-start(pred[128]{0:T(512)(128)(4,1)S(1)} %get-tuple-element.50) | copy-start | bytes 388
  3.3 71.2 %copy-start.45 = (f32[128]{0:T(128)}, f32[128]{0:T(128)S(1)}, u32[]{:S(2)}) copy-start(f32[128]{0:T(128)S(1)} %get-tuple-element.51) | copy-start | bytes 1540
  3.3 71.2 %copy-start.47 = (f32[128]{0:T(128)}, f32[128]{0:T(128)S(1)}, u32[]{:S(2)}) copy-start(f32[128]{0:T(128)S(1)} %get-tuple-element.52) | copy-start | bytes 1540
  3.3 71.2 %copy-start.49 = (f32[128]{0:T(128)}, f32[128]{0:T(128)S(1)}, u32[]{:S(2)}) copy-start(f32[128]{0:T(128)S(1)} %get-tuple-element.53) | copy-start | bytes 1540
  4.2 77.5 %copy-start.35 = (pred[128,128]{1,0:T(8,128)(4,1)}, pred[128,128]{1,0:T(8,128)(4,1)S(1)}, u32[]{:S(2)}) copy-start(pred[128,128]{1,0:T(8,128)(4,1)S(1)} %fusion.49) | copy-start | bytes 49156
  56.1 3.0 %copy-start = (bf16[4,2,2,2,920,128]{5,4,3,2,1,0:T(8,128)(2,1)}, bf16[4,2,2,2,920,128]{5,4,3,2,1,0:T(8,128)(2,1)S(1)}, u32[]{:S(2)}) copy-start(bf16[4,2,2,2,920,128]{5,4,3,2,1,0:T(8,128)(2,1)S(1)} %shard_map.118) | copy-start | bytes 22609924
  56.2 18.3 %copy-start.21 = (f32[1792]{0:T(1024)}, f32[1792]{0:T(1024)S(1)}, u32[]{:S(2)}) copy-start(f32[1792]{0:T(1024)S(1)} %get-tuple-element.45) | copy-start | bytes 21508
  56.2 18.3 %copy-start.23 = (f32[1792]{0:T(1024)}, f32[1792]{0:T(1024)S(1)}, u32[]{:S(2)}) copy-start(f32[1792]{0:T(1024)S(1)} %get-tuple-element.46) | copy-start | bytes 21508
  56.2 18.3 %copy-start.25 = (f32[1792]{0:T(1024)}, f32[1792]{0:T(1024)S(1)}, u32[]{:S(2)}) copy-start(f32[1792]{0:T(1024)S(1)} %get-tuple-element.48) | copy-start | bytes 21508
  56.2 18.3 %copy-start.27 = (f32[1792]{0:T(1024)}, f32[1792]{0:T(1024)S(1)}, u32[]{:S(2)}) copy-start(f32[1792]{0:T(1024)S(1)} %get-tuple-element.47) | copy-start | bytes 21508
  59.1 10.6 %copy-start.29 = (bf16[29056]{0:T(1024)(128)(2,1)}, bf16[29056]{0:T(1024)(128)(2,1)S(1)}, u32[]{:S(2)}) copy-start(bf16[29056]{0:T(1024)(128)(2,1)S(1)} %slice_bitcast_fusion) | copy-start | bytes 174340
  59.1 11.0 %copy-start.12 = (bf16[128,768]{1,0:T(8,128)(2,1)S(1)}, bf16[128,768]{1,0:T(8,128)(2,1)}, u32[]{:S(2)}) copy-start(bf16[128,768]{1,0:T(8,128)(2,1)} %param.7) | copy-start | bytes 589828
  69.7 4.6 %copy-start.52 = (f32[24]{0:T(128)}, f32[24]{0:T(128)S(1)}, u32[]{:S(2)}) copy-start(f32[24]{0:T(128)S(1)} %fusion.73) | copy-start | bytes 292
  69.7 11.9 %copy-start.58 = (f32[24]{0:T(128)}, f32[24]{0:T(128)S(1)}, u32[]{:S(2)}) copy-start(f32[24]{0:T(128)S(1)} %get-tuple-element.43) | copy-start | bytes 292
  69.8 19.9 %copy-start.20 = (f32[1536]{0:T(1024)}, f32[1536]{0:T(1024)S(1)}, u32[]{:S(2)}) copy-start(f32[1536]{0:T(1024)S(1)} %slice_convert_fusion.1) | copy-start | bytes 18436
  70.5 11.2 %copy-start.37 = (f32[24,128]{1,0:T(8,128)}, f32[24,128]{1,0:T(8,128)S(1)}, u32[]{:S(2)}) copy-start(f32[24,128]{1,0:T(8,128)S(1)} %get-tuple-element.54) | copy-start | bytes 36868
  70.9 10.8 %copy-start.39 = (f32[24,128]{1,0:T(8,128)}, f32[24,128]{1,0:T(8,128)S(1)}, u32[]{:S(2)}) copy-start(f32[24,128]{1,0:T(8,128)S(1)} %copy.50) | copy-start | bytes 36868
  74.2 1.2 copy-start.1
  74.3 1.4 copy-start.7
  74.4 3.0 %copy-start.3 = (f32[126,1792]{1,0:T(8,128)}, f32[126,1792]{1,0:T(8,128)S(1)}, u32[]{:S(2)}) copy-start(f32[126,1792]{1,0:T(8,128)S(1)} %slice.117) | copy-start | bytes 2709508
  75.8 1.6 copy-start.5
  77.4 0.9 copy-start.9
  78.3 3.4 %copy-start.30 = (f32[128,128]{1,0:T(8,128)}, f32[128,128]{1,0:T(8,128)S(1)}, u32[]{:S(2)}) copy-start(f32[128,128]{1,0:T(8,128)S(1)} %fusion.52) | copy-start | bytes 196612
  89.7 1.6 copy-start.10
  89.7 1.6 copy-start.11
  96.1 2.9 %copy-start.17 = (f32[128,1536]{0,1:T(8,128)S(1)}, f32[128,1536]{0,1:T(8,128)}, u32[]{:S(2)}) copy-start(f32[128,1536]{0,1:T(8,128)} %copy.48) | copy-start | bytes 2359300
  96.1 2.9 %copy-start.31 = (f32[128,128]{1,0:T(8,128)S(1)}, f32[128,128]{1,0:T(8,128)}, u32[]{:S(2)}) copy-start(f32[128,128]{1,0:T(8,128)} %copy-done.30) | copy-start | bytes 196612
  96.1 2.9 %copy-start.36 = (pred[128,128]{1,0:T(8,128)(4,1)S(1)}, pred[128,128]{1,0:T(8,128)(4,1)}, u32[]{:S(2)}) copy-start(pred[128,128]{1,0:T(8,128)(4,1)} %copy-done.35) | copy-start | bytes 49156
  96.1 2.9 %copy-start.38 = (f32[24,128]{1,0:T(8,128)S(1)}, f32[24,128]{1,0:T(8,128)}, u32[]{:S(2)}) copy-start(f32[24,128]{1,0:T(8,128)} %copy-done.37) | copy-start | bytes 36868
  96.1 2.9 %copy-start.40 = (f32[24,128]{1,0:T(8,128)S(1)}, f32[24,128]{1,0:T(8,128)}, u32[]{:S(2)}) copy-start(f32[24,128]{1,0:T(8,128)} %copy-done.39) | copy-start | bytes 36868
  99.0 2.8 %copy-start.59 = (f32[24]{0:T(128)S(1)}, f32[24]{0:T(128)}, u32[]{:S(2)}) copy-start(f32[24]{0:T(128)} %copy-done.58) | copy-start | bytes 292
  102.9 2.5 %copy-start.53 = (f32[24]{0:T(128)S(1)}, f32[24]{0:T(128)}, u32[]{:S(2)}) copy-start(f32[24]{0:T(128)} %copy-done.52) | copy-start | bytes 292
  102.9 6.6 %copy-start.8 = (f32[125,1792]{1,0:T(8,128)S(1)}, f32[125,1792]{1,0:T(8,128)}, u32[]{:S(2)}) copy-start(f32[125,1792]{1,0:T(8,128)} %copy-done.7) | copy-start | bytes 2688004
  102.9 6.6 %copy-start.50 = (f32[128]{0:T(128)S(1)}, f32[128]{0:T(128)}, u32[]{:S(2)}) copy-start(f32[128]{0:T(128)} %copy-done.49) | copy-start | bytes 1540
  106.2 7.9 %copy-start.32 = (bf16[128,24]{0,1:T(8,128)(2,1)}, bf16[128,24]{0,1:T(8,128)(2,1)S(1)}, u32[]{:S(2)}) copy-start(bf16[128,24]{0,1:T(8,128)(2,1)S(1)} %get-tuple-element.26) | copy-start | bytes 18436
  109.6 3.0 %copy-start.4 = (f32[126,1792]{1,0:T(8,128)S(1)}, f32[126,1792]{1,0:T(8,128)}, u32[]{:S(2)}) copy-start(f32[126,1792]{1,0:T(8,128)} %copy-done.3) | copy-start | bytes 2709508
  109.6 3.0 %copy-start.6 = (f32[127,1792]{1,0:T(8,128)S(1)}, f32[127,1792]{1,0:T(8,128)}, u32[]{:S(2)}) copy-start(f32[127,1792]{1,0:T(8,128)} %copy-done.5) | copy-start | bytes 2731012
  109.6 3.0 %copy-start.46 = (f32[128]{0:T(128)S(1)}, f32[128]{0:T(128)}, u32[]{:S(2)}) copy-start(f32[128]{0:T(128)} %copy-done.45) | copy-start | bytes 1540
  109.6 3.0 %copy-start.48 = (f32[128]{0:T(128)S(1)}, f32[128]{0:T(128)}, u32[]{:S(2)}) copy-start(f32[128]{0:T(128)} %copy-done.47) | copy-start | bytes 1540
  112.6 1.9 %copy-start.28 = (f32[1792]{0:T(1024)S(1)}, f32[1792]{0:T(1024)}, u32[]{:S(2)}) copy-start(f32[1792]{0:T(1024)} %copy-done.27) | copy-start | bytes 21508
  114.0 1.9 %copy-start.26 = (f32[1792]{0:T(1024)S(1)}, f32[1792]{0:T(1024)}, u32[]{:S(2)}) copy-start(f32[1792]{0:T(1024)} %copy-done.25) | copy-start | bytes 21508
  114.5 1.5 copy-start.14
  114.5 1.5 copy-start.24
  115.9 1.5 copy-start.2
  115.9 1.5 copy-start.22
  117.4 0.7 copy-start.34
  117.4 0.7 copy-start.51
  117.4 0.7 copy-start.54
  117.4 0.7 copy-start.57
  119.4 4.3 %copy-start.33 = (bf16[128,24]{0,1:T(8,128)(2,1)S(1)}, bf16[128,24]{0,1:T(8,128)(2,1)}, u32[]{:S(2)}) copy-start(bf16[128,24]{0,1:T(8,128)(2,1)} %copy-done.32) | copy-start | bytes 18436
  119.4 4.3 %copy-start.42 = (f32[128]{0:T(128)S(1)}, f32[128]{0:T(128)}, u32[]{:S(2)}) copy-start(f32[128]{0:T(128)} %copy-done.41) | copy-start | bytes 1540
  119.4 4.7 %copy-start.56 = (f32[128]{0:T(128)S(1)}, f32[128]{0:T(128)}, u32[]{:S(2)}) copy-start(f32[128]{0:T(128)} %copy-done.55) | copy-start | bytes 1540
  119.4 4.7 %copy-start.16 = (bf16[128,768]{1,0:T(8,128)(2,1)S(1)}, bf16[128,768]{1,0:T(8,128)(2,1)}, u32[]{:S(2)}) copy-start(bf16[128,768]{1,0:T(8,128)(2,1)} %param.8) | copy-start | bytes 589828
  119.4 4.7 %copy-start.44 = (pred[128]{0:T(512)(128)(4,1)S(1)}, pred[128]{0:T(512)(128)(4,1)}, u32[]{:S(2)}) copy-start(pred[128]{0:T(512)(128)(4,1)} %copy-done.43) | copy-start | bytes 388
  132.2 50.4 %copy-start.15 = (f32[117760]{0:T(1024)S(1)}, f32[117760]{0:T(1024)}, u32[]{:S(2)}) copy-start(f32[117760]{0:T(1024)} %param.10) | copy-start | bytes 1413124
  132.2 50.4 %copy-start.18 = (f32[117760]{0:T(1024)S(1)}, f32[117760]{0:T(1024)}, u32[]{:S(2)}) copy-start(f32[117760]{0:T(1024)} %param.12) | copy-start | bytes 1413124
  132.2 50.4 %copy-start.19 = (f32[117760]{0:T(1024)S(1)}, f32[117760]{0:T(1024)}, u32[]{:S(2)}) copy-start(f32[117760]{0:T(1024)} %param.11) | copy-start | bytes 1413124
  182.6 2.4 %copy-start.13 = (f32[920,128]{1,0:T(8,128)S(1)}, f32[920,128]{1,0:T(8,128)}, u32[]{:S(2)}) copy-start(f32[920,128]{1,0:T(8,128)} %shard_map.121) | copy-start | bytes 1413124
